TPU v7x, 128 devices: a whole 4x4x4 slice. The times are simulated.
128 devices in a mesh: wide: 16 (over z_hi, x, core), narrow: 8 (over y, z_lo).
Axes of the slice: x: 4, y: 4, z: 4 (z_hi: 2, z_lo: 2; z = z_hi * 2 + z_lo), core: 2. Of those that a mesh axis runs over, the one named last changes fastest.
Arguments:
- hidden: bfloat16 [4096, 14336], P('narrow', 'wide'), may hold values from -6 to 6
- out_grad: bfloat16 [4096, 4096], P('wide', 'narrow'), may hold values from -6 to 6
- sign_bits: int32 [14336, 4096], P('wide', 'narrow'), may hold values 0 or 1
- pick_rows: int32 [8192], replicated, may hold values from 0 to 14335
- pick_cols: int32 [8192], replicated, may hold values from 0 to 4095
Outputs:
- sketch: float32 [2, 8192], replicated
All inputs are finite; a program needn't handle non-finite values. No bound on the sum of `sign_bits` on one device may be relied on, other than what follows from the above.
Results may differ from a plain program's by a relative error of at most 0.0003.
Values may be sent and summed in bfloat16 or wider, within the bound.
A program may use at most 64 MiB of HBM per device.

v0:
```python
import math

import jax
import jax.numpy as jnp
from jax import lax
from jax.sharding import PartitionSpec as P

EXAMPLES = 2
SEQ = 2048
GROUPS = 16
BAND = 128


def from_partner(block, axis, bit):
    count = lax.axis_size(axis)
    route = []
    for low in range(count):
        high = low | 1 << bit
        if high != low and high < count:
            route += [(low, high), (high, low)]
    return lax.ppermute(block, axis, route)


def bit_parity(value, count):
    total = jnp.zeros_like(value)
    for bit_num in range(count):
        total = total + jnp.bitwise_and(jnp.right_shift(value, bit_num), 1)
    return total % 2


def walsh_table(length):
    numbers = lax.iota(jnp.int32, length)
    parity = bit_parity(
        jnp.bitwise_and(numbers[:, None], numbers[None, :]), length.bit_length() - 1
    )
    return (1 - 2 * parity).astype(jnp.float32) / math.sqrt(length)


def shards(hidden, out_grad, sign_bits, pick_rows, pick_cols):
    acts_all = lax.all_gather(hidden, "narrow", axis=0, tiled=True)
    grads_all = lax.all_gather(out_grad, "wide", axis=0, tiled=True)
    rows_local = acts_all.shape[1]
    cols_local = grads_all.shape[1]
    acts_all = acts_all.reshape(EXAMPLES, -1, rows_local)
    grads_all = grads_all.reshape(EXAMPLES, -1, cols_local)
    gradient = jnp.einsum("esr,esc->erc", acts_all, grads_all, preferred_element_type=jnp.float32)
    flipped = gradient * (2 * sign_bits - 1).astype(jnp.float32)[None]
    wide_count = lax.axis_size("wide")
    narrow_count = lax.axis_size("narrow")
    groups_local = GROUPS // wide_count
    middle = rows_local // (groups_local * BAND)
    blocks = flipped.reshape(EXAMPLES, groups_local, middle, BAND, cols_local)
    blocks = jnp.einsum(
        "ehmpc,gh->egmpc", blocks, walsh_table(groups_local), precision=lax.Precision.HIGHEST
    )
    blocks = jnp.einsum(
        "ehmpc,qp->ehmqc", blocks, walsh_table(BAND), precision=lax.Precision.HIGHEST
    )
    blocks = jnp.dot(
        blocks.reshape(-1, cols_local), walsh_table(cols_local), precision=lax.Precision.HIGHEST
    )
    local = blocks.reshape(EXAMPLES, rows_local * cols_local)
    position = pick_rows % rows_local * cols_local + pick_cols % cols_local
    row_owner = pick_rows // rows_local
    col_owner = pick_cols // cols_local
    wide_index = lax.axis_index("wide")
    narrow_index = lax.axis_index("narrow")
    halving = 1.0 / math.sqrt(2.0)
    for bit_num in range(wide_count.bit_length() - 1):
        partner = from_partner(local, "wide", bit_num)
        upper = jnp.bitwise_and(jnp.right_shift(wide_index, bit_num), 1) == 1
        local = jnp.where(upper, partner - local, local + partner) * halving
    for bit_num in range(narrow_count.bit_length() - 1):
        partner = from_partner(local, "narrow", bit_num)
        upper = jnp.bitwise_and(jnp.right_shift(narrow_index, bit_num), 1) == 1
        local = jnp.where(upper, partner - local, local + partner) * halving
    picked = local[:, position]
    owned = (row_owner == wide_index) & (col_owner == narrow_index)
    terms = jnp.where(owned[None, :], picked, 0.0)
    terms = terms * (1.0 / math.sqrt(SEQ))
    return lax.psum(terms, ("wide", "narrow"))


def solution(mesh):
    placed = (P("narrow", "wide"), P("wide", "narrow"), P("wide", "narrow"), P(), P())
    return jax.shard_map(shards, mesh=mesh, in_specs=placed, out_specs=P(), check_vma=False)
```

profile of v0, /device:TPU:1, one launch (start us, length us, event | category | flops | bytes accessed | tf_op | source)
XLA Modules:
  0.0 1026.6 jit_solution(13222279830555741180)
XLA Ops:
  6.5 0.0 all-gather.5.cloned.1.call-start
  6.5 0.7 all-gather.5.cloned.1.call-update
  7.3 0.0 all-gather.3.cloned.1.call-start
  7.3 0.7 all-gather.3.cloned.1.call-update
  8.0 0.0 all-reduce.2.cloned.1.call-start
  8.1 1.7 add_convert_fusion
  9.8 59.8 %all-gather.5.cloned.1.call-done = bf16[4096,512]{1,0:T(8,128)(2,1)} async-done(((bf16[256,512]{1,0:T(8,128)(2,1)}), bf16[4096,512]{1,0:T(8,128)(2,1)}) %all-gather.5.cloned.1.call-update) | async-done | bytes 4194320 | tf_op jit(solution)/shard_map/all_gather | solution.py:41
  69.6 148.4 %all-gather.3.cloned.1.call-done = bf16[4096,896]{1,0:T(8,128)(2,1)} async-done(((bf16[512,896]{1,0:T(8,128)(2,1)}), bf16[4096,896]{1,0:T(8,128)(2,1)}) %all-gather.3.cloned.1.call-update) | async-done | bytes 7340048 | tf_op jit(solution)/shard_map/all_gather | solution.py:40
  218.0 9.8 convolution_multiply_fusion
  227.8 3.5 fusion.26
  231.3 9.4 fusion.5
  240.7 7.2 reshape.26
  247.9 0.8 collective-permute-start
  248.7 6.4 collective-permute-done
  255.1 6.4 select_multiply_fusion.6
  261.5 1.2 collective-permute-start.1
  262.7 79.6 %collective-permute-done.1 = f32[2,458752]{1,0:T(2,128)} collective-permute-done((f32[2,458752]{1,0:T(2,128)}, f32[2,458752]{1,0:T(2,128)}, u32[]{:S(2)}, u32[]{:S(2)}) %collective-permute-start.1) | collective-permute-done | bytes 3670048 | tf_op jit(solution)/shard_map/ppermute | solution.py:21
  342.4 6.4 select_multiply_fusion.5
  348.8 2.7 collective-permute-start.2
  351.5 78.8 %collective-permute-done.2 = f32[2,458752]{1,0:T(2,128)} collective-permute-done((f32[2,458752]{1,0:T(2,128)}, f32[2,458752]{1,0:T(2,128)}, u32[]{:S(2)}, u32[]{:S(2)}) %collective-permute-start.2) | collective-permute-done | bytes 3670048 | tf_op jit(solution)/shard_map/ppermute | solution.py:21
  430.3 6.4 select_multiply_fusion.4
  436.7 2.6 collective-permute-start.3
  439.3 78.1 %collective-permute-done.3 = f32[2,458752]{1,0:T(2,128)} collective-permute-done((f32[2,458752]{1,0:T(2,128)}, f32[2,458752]{1,0:T(2,128)}, u32[]{:S(2)}, u32[]{:S(2)}) %collective-permute-start.3) | collective-permute-done | bytes 3670048 | tf_op jit(solution)/shard_map/ppermute | solution.py:21
  517.3 6.4 select_multiply_fusion.3
  523.7 0.0 collective-permute-start.4
  523.8 78.3 %collective-permute-done.4 = f32[2,458752]{1,0:T(2,128)} collective-permute-done((f32[2,458752]{1,0:T(2,128)}, f32[2,458752]{1,0:T(2,128)}, u32[]{:S(2)}, u32[]{:S(2)}) %collective-permute-start.4) | collective-permute-done | bytes 3670048 | tf_op jit(solution)/shard_map/ppermute | solution.py:21
  602.0 6.4 select_multiply_fusion.2
  608.4 3.1 collective-permute-start.5
  611.5 0.0 copy-start
  611.5 0.0 copy-start.1
  611.5 76.5 %collective-permute-done.5 = f32[2,458752]{1,0:T(2,128)} collective-permute-done((f32[2,458752]{1,0:T(2,128)}, f32[2,458752]{1,0:T(2,128)}, u32[]{:S(2)}, u32[]{:S(2)}) %collective-permute-start.5) | collective-permute-done | bytes 3670048 | tf_op jit(solution)/shard_map/ppermute | solution.py:21
  688.0 6.4 select_multiply_fusion.1
  694.4 4.6 collective-permute-start.6
  699.0 0.0 copy-done
  699.0 0.0 copy-done.1
  699.0 0.1 fusion.46
  699.1 75.3 %collective-permute-done.6 = f32[2,458752]{1,0:T(2,128)} collective-permute-done((f32[2,458752]{1,0:T(2,128)}, f32[2,458752]{1,0:T(2,128)}, u32[]{:S(2)}, u32[]{:S(2)}) %collective-permute-start.6) | collective-permute-done | bytes 3670048 | tf_op jit(solution)/shard_map/ppermute | solution.py:21
  774.4 6.4 select_multiply_fusion
  780.8 91.3 %gather_fusion = f32[8192,2]{0,1:T(2,128)S(1)} fusion(f32[2,458752]{1,0:T(2,128)} %select_multiply_fusion, s32[8192]{0:T(1024)S(1)} %fusion.35), kind=kCustom, calls=%fused_computation | custom fusion | bytes 163840 | tf_op jit(solution)/shard_map/gather | solution.py:77
  872.2 0.7 multiply_bitcast_fusion
  872.8 0.0 all-reduce.2.cloned.1.call-update
  872.9 145.7 %all-reduce.2.cloned.1.call-done = f32[2,8192]{1,0:T(2,128)} async-done(((f32[2,8192]{1,0:T(2,128)}), f32[2,8192]{1,0:T(2,128)}) %all-reduce.2.cloned.1.call-update) | async-done | bytes 65552 | tf_op jit(solution)/shard_map/psum | solution.py:81
  1018.6 1.5 copy.10
  (1 shorter events, 0.0 us)
Async XLA Ops:
  6.5 63.0 %all-gather.5.cloned.1.call-start = ((), (), s32[]{:S(2)}) async-start(), calls=%async_computation.1 | async-start | bytes 4456448 | tf_op jit(solution)/shard_map/all_gather | solution.py:41
  7.3 210.7 %all-gather.3.cloned.1.call-start = ((), (), s32[]{:S(2)}) async-start(), calls=%async_computation | async-start | bytes 8257536 | tf_op jit(solution)/shard_map/all_gather | solution.py:40
  8.0 1010.6 %all-reduce.2.cloned.1.call-start = ((), (), s32[]{:S(2)}) async-start(), calls=%async_computation.2 | async-start | bytes 131072 | tf_op jit(solution)/shard_map/psum | solution.py:81
  247.9 7.2 collective-permute-start
  261.5 80.8 %collective-permute-start.1 = (f32[2,458752]{1,0:T(2,128)}, f32[2,458752]{1,0:T(2,128)}, u32[]{:S(2)}, u32[]{:S(2)}) collective-permute-start(f32[2,458752]{1,0:T(2,128)} %select_multiply_fusion.6), channel_id=1, source_target_pairs={{0,16},{16,0},{8,24},{24,8},{32,48},{48,32},{40,56},{56,40},{64,80... | collective-permute-start | bytes 11010056 | tf_op jit(solution)/shard_map/ppermute | solution.py:21
  348.8 81.5 %collective-permute-start.2 = (f32[2,458752]{1,0:T(2,128)}, f32[2,458752]{1,0:T(2,128)}, u32[]{:S(2)}, u32[]{:S(2)}) collective-permute-start(f32[2,458752]{1,0:T(2,128)} %select_multiply_fusion.5), channel_id=1, source_target_pairs={{0,32},{32,0},{8,40},{40,8},{16,48},{48,16},{24,56},{56,24},{64,96... | collective-permute-start | bytes 11010056 | tf_op jit(solution)/shard_map/ppermute | solution.py:21
  436.7 80.6 %collective-permute-start.3 = (f32[2,458752]{1,0:T(2,128)}, f32[2,458752]{1,0:T(2,128)}, u32[]{:S(2)}, u32[]{:S(2)}) collective-permute-start(f32[2,458752]{1,0:T(2,128)} %select_multiply_fusion.4), channel_id=1, source_target_pairs={{0,64},{64,0},{8,72},{72,8},{16,80},{80,16},{24,88},{88,24},{32,96... | collective-permute-start | bytes 11010056 | tf_op jit(solution)/shard_map/ppermute | solution.py:21
  523.7 78.3 %collective-permute-start.4 = (f32[2,458752]{1,0:T(2,128)}, f32[2,458752]{1,0:T(2,128)}, u32[]{:S(2)}, u32[]{:S(2)}) collective-permute-start(f32[2,458752]{1,0:T(2,128)} %select_multiply_fusion.3), channel_id=1, source_target_pairs={{0,1},{1,0},{2,3},{3,2},{4,5},{5,4},{6,7},{7,6},{8,9},{9,8},{10,11... | collective-permute-start | bytes 11010056 | tf_op jit(solution)/shard_map/ppermute | solution.py:21
  608.4 79.6 %collective-permute-start.5 = (f32[2,458752]{1,0:T(2,128)}, f32[2,458752]{1,0:T(2,128)}, u32[]{:S(2)}, u32[]{:S(2)}) collective-permute-start(f32[2,458752]{1,0:T(2,128)} %select_multiply_fusion.2), channel_id=1, source_target_pairs={{0,2},{2,0},{1,3},{3,1},{4,6},{6,4},{5,7},{7,5},{8,10},{10,8},{9,1... | collective-permute-start | bytes 11010056 | tf_op jit(solution)/shard_map/ppermute | solution.py:21
  611.5 87.5 %copy-start = (s32[8192]{0:T(1024)S(1)}, s32[8192]{0:T(1024)}, u32[]{:S(2)}) copy-start(s32[8192]{0:T(1024)} %param.8) | copy-start | bytes 98308
  611.5 87.5 %copy-start.1 = (s32[8192]{0:T(1024)S(1)}, s32[8192]{0:T(1024)}, u32[]{:S(2)}) copy-start(s32[8192]{0:T(1024)} %param.9) | copy-start | bytes 98308
  694.4 80.0 %collective-permute-start.6 = (f32[2,458752]{1,0:T(2,128)}, f32[2,458752]{1,0:T(2,128)}, u32[]{:S(2)}, u32[]{:S(2)}) collective-permute-start(f32[2,458752]{1,0:T(2,128)} %select_multiply_fusion.1), channel_id=1, source_target_pairs={{0,4},{4,0},{1,5},{5,1},{2,6},{6,2},{3,7},{7,3},{8,12},{12,8},{9,1... | collective-permute-start | bytes 11010056 | tf_op jit(solution)/shard_map/ppermute | solution.py:21
Sparse Core Ops, SparseCore 0:
  9.8 59.7 all-gather.4
  71.2 146.7 all-gather.2
  873.0 145.5 all-reduce.1
where the time goes:
time: 1030 us
  waiting for transfers between devices  828 us (80%)
  local copies, waits for them, and re-layouts  100 us (10%)
  other arithmetic  47.4 us (5%)
  matrix products  22.7 us (2%)
  starting transfers between devices  15 us (1%)
  between operations  13.2 us (1%)
    ppermute x7, waiting for transfers between devices, from_partner(): return lax.ppermute(block, axis, route)  473 us
    all_gather x1, waiting for transfers between devices, shards(): acts_all = lax.all_gather(hidden, 'narrow', axis=0, tiled=True)  148 us
    psum x1, waiting for transfers between devices, shards(): return lax.psum(terms, ('wide', 'narrow'))  146 us
    gather x1, local copies, waits for them, and re-layouts, shards(): picked = local[:, position]  91.3 us
    all_gather x1, waiting for transfers between devices, shards(): grads_all = lax.all_gather(out_grad, 'wide', axis=0, tiled=True)  59.8 us
    mul x7, other arithmetic, shards(): local = jnp.where(upper, partner - local, local + partner) * halving  44.9 us
  transfers between devices with their start and end apart: 10, of which 10 were waited for; matrix products, arithmetic and copies ran while one was open for 0% of the time, Pallas kernels for 0%

commit v1 on v0

--- a/solution.py
+++ b/solution.py
@@ -9,16 +9,6 @@
 SEQ = 2048
 GROUPS = 16
 BAND = 128
-
-
-def from_partner(block, axis, bit):
-    count = lax.axis_size(axis)
-    route = []
-    for low in range(count):
-        high = low | 1 << bit
-        if high != low and high < count:
-            route += [(low, high), (high, low)]
-    return lax.ppermute(block, axis, route)
 
 
 def bit_parity(value, count):
@@ -65,19 +55,12 @@
     col_owner = pick_cols // cols_local
     wide_index = lax.axis_index("wide")
     narrow_index = lax.axis_index("narrow")
-    halving = 1.0 / math.sqrt(2.0)
-    for bit_num in range(wide_count.bit_length() - 1):
-        partner = from_partner(local, "wide", bit_num)
-        upper = jnp.bitwise_and(jnp.right_shift(wide_index, bit_num), 1) == 1
-        local = jnp.where(upper, partner - local, local + partner) * halving
-    for bit_num in range(narrow_count.bit_length() - 1):
-        partner = from_partner(local, "narrow", bit_num)
-        upper = jnp.bitwise_and(jnp.right_shift(narrow_index, bit_num), 1) == 1
-        local = jnp.where(upper, partner - local, local + partner) * halving
     picked = local[:, position]
-    owned = (row_owner == wide_index) & (col_owner == narrow_index)
-    terms = jnp.where(owned[None, :], picked, 0.0)
-    terms = terms * (1.0 / math.sqrt(SEQ))
+    flips = bit_parity(
+        jnp.bitwise_and(row_owner, wide_index), wide_count.bit_length() - 1
+    ) + bit_parity(jnp.bitwise_and(col_owner, narrow_index), narrow_count.bit_length() - 1)
+    scale = 1.0 / math.sqrt(SEQ * wide_count * narrow_count)
+    terms = picked * ((1 - 2 * (flips % 2)).astype(jnp.float32) * scale)[None, :]
     return lax.psum(terms, ("wide", "narrow"))
 
 

time: 1030 us -> 495 us (0.48)
  waiting for transfers between devices: 828 us -> 353 us
  other arithmetic: 47.4 us -> 4.12 us
  starting transfers between devices: 15 us -> 0.08 us
    ppermute x7 -> x0, waiting for transfers between devices: 473 us -> none  [from_partner(): return lax.ppermute(block, axis, route)]
    mul x8 -> x2, other arithmetic: 45.6 us -> 1.56 us  [the longest x1 0.9 us: shards(): (1 - 2 * (flips % 2)).astype(jnp.float32) * scale]
    ppermute x7 -> x0, starting transfers between devices: 15 us -> none  [from_partner(): return lax.ppermute(block, axis, route)]
  transfers between devices with their start and end apart: 10 -> 3, of which waited for: 10 -> 3; matrix products, arithmetic and copies ran while one was open for 0% -> 1% of each run, Pallas kernels for 0% -> 0%
where the time goes in v1:
time: 495 us; the launch traced here: 493 us
  waiting for transfers between devices  353 us (71%)
  local copies, waits for them, and re-layouts  99.9 us (20%)
  matrix products  22.5 us (5%)
  between operations  13.1 us (3%)
    all_gather x1, waiting for transfers between devices, shards(): acts_all = lax.all_gather(hidden, 'narrow', axis=0, tiled=True)  148 us
    psum x1, waiting for transfers between devices, shards(): return lax.psum(terms, ('wide', 'narrow'))  145 us
    gather x1, local copies, waits for them, and re-layouts, shards(): picked = local[:, position]  91.2 us
    all_gather x1, waiting for transfers between devices, shards(): grads_all = lax.all_gather(out_grad, 'wide', axis=0, tiled=True)  58.1 us
  transfers between devices with their start and end apart: 3, of which 3 were waited for; matrix products, arithmetic and copies ran while one was open for 1% of the time, Pallas kernels for 0%

profile of v1, /device:TPU:1, one launch (start us, length us, event | category | flops | bytes accessed | tf_op | source)
XLA Modules:
  0.0 492.8 jit_solution(172012672987805331)
XLA Ops:
  6.5 0.0 all-gather.5.cloned.1.call-start
  6.5 0.7 all-gather.5.cloned.1.call-update
  7.3 0.0 all-gather.3.cloned.1.call-start
  7.3 0.7 all-gather.3.cloned.1.call-update
  8.0 0.0 all-reduce.2.cloned.1.call-start
  8.1 0.8 fusion.43
  8.9 0.9 fusion.42
  9.8 1.7 add_convert_fusion
  11.5 58.1 %all-gather.5.cloned.1.call-done = bf16[4096,512]{1,0:T(8,128)(2,1)} async-done(((bf16[256,512]{1,0:T(8,128)(2,1)}), bf16[4096,512]{1,0:T(8,128)(2,1)}) %all-gather.5.cloned.1.call-update) | async-done | bytes 4194320 | tf_op jit(solution)/shard_map/all_gather | solution.py:31
  69.6 148.4 %all-gather.3.cloned.1.call-done = bf16[4096,896]{1,0:T(8,128)(2,1)} async-done(((bf16[512,896]{1,0:T(8,128)(2,1)}), bf16[4096,896]{1,0:T(8,128)(2,1)}) %all-gather.3.cloned.1.call-update) | async-done | bytes 7340048 | tf_op jit(solution)/shard_map/all_gather | solution.py:30
  218.0 9.8 %convolution_multiply_fusion = f32[2,896,512]{2,1,0:T(8,128)S(1)} fusion(bf16[2,2048,896]{2,1,0:T(8,128)(2,1)} %bitcast.21, bf16[2,2048,512]{2,1,0:T(8,128)(2,1)} %bitcast.22, f32[896,512]{1,0:T(8,128)S(1)} %add_convert_fusion), kind=kOutput, calls=%fused_computation.1 | convolution fusion | flops 3759013888 | bytes 17039360 | tf_op jit(solution)/shard_map/esr,esc->erc/dot_general | solution.py:36
  227.8 3.4 fusion.26
  231.2 9.3 %fusion.5 = f32[1792,512]{1,0:T(8,128)} fusion(f32[1792,512]{1,0:T(8,128)S(1)} %bitcast.20), kind=kOutput, calls=%fused_computation.11 | convolution fusion | flops 5648154624 | bytes 7340032 | tf_op jit(solution)/shard_map/dot_general | solution.py:49
  240.5 7.2 %reshape.26 = f32[2,458752]{1,0:T(2,128)} reshape(f32[1792,512]{1,0:T(8,128)} %fusion.5) | data formatting | bytes 7340032 | tf_op jit(solution)/shard_map/reshape | solution.py:52
  247.7 91.2 %gather_fusion = f32[8192,2]{0,1:T(2,128)S(1)} fusion(f32[2,458752]{1,0:T(2,128)} %reshape.26, s32[8192]{0:T(1024)S(1)} %fusion.43), kind=kCustom, calls=%fused_computation | custom fusion | bytes 163840 | tf_op jit(solution)/shard_map/gather | solution.py:58
  339.0 0.7 multiply_bitcast_fusion
  339.7 0.0 all-reduce.2.cloned.1.call-update
  339.7 145.1 %all-reduce.2.cloned.1.call-done = f32[2,8192]{1,0:T(2,128)} async-done(((f32[2,8192]{1,0:T(2,128)}), f32[2,8192]{1,0:T(2,128)}) %all-reduce.2.cloned.1.call-update) | async-done | bytes 65552 | tf_op jit(solution)/shard_map/psum | solution.py:64
  484.8 1.5 copy.10
Async XLA Ops:
  6.5 63.0 %all-gather.5.cloned.1.call-start = ((), (), s32[]{:S(2)}) async-start(), calls=%async_computation.1 | async-start | bytes 4456448 | tf_op jit(solution)/shard_map/all_gather | solution.py:31
  7.3 210.7 %all-gather.3.cloned.1.call-start = ((), (), s32[]{:S(2)}) async-start(), calls=%async_computation | async-start | bytes 8257536 | tf_op jit(solution)/shard_map/all_gather | solution.py:30
  8.0 476.7 %all-reduce.2.cloned.1.call-start = ((), (), s32[]{:S(2)}) async-start(), calls=%async_computation.2 | async-start | bytes 131072 | tf_op jit(solution)/shard_map/psum | solution.py:64
Sparse Core Ops, SparseCore 0:
  9.8 59.7 all-gather.4
  71.2 146.7 all-gather.2
  339.8 144.9 all-reduce.1

commit v2 on v1

v2 whole, which is shorter than its diff:
```python
import math

import jax
import jax.numpy as jnp
from jax import lax
from jax.experimental import pallas as pl
from jax.experimental.pallas import tpu as pltpu
from jax.sharding import PartitionSpec as P

SEQ = 2048
BAND = 128
LANES = 128
WIDE = 16
NARROW = 8
MESH = pl.DeviceIdType.MESH


def bit_parity(value, count):
    total = jnp.zeros_like(value)
    for bit_num in range(count):
        total = total + jnp.bitwise_and(jnp.right_shift(value, bit_num), 1)
    return jnp.bitwise_and(total, 1)


def place():
    wide, narrow = lax.axis_index("wide"), lax.axis_index("narrow")
    return wide // 8, (wide // 2) % 4, wide % 2, narrow // 2, narrow % 2


def device(z_hi, x, core, y, z_lo):
    return (z_hi * 8 + x * 2 + core, y * 2 + z_lo)


def transform_kernel(
    acts, grads, signs, out, hbuf, gbuf, sbuf, total,
    local_sem, hy_send, hz_send, h_recv, init_send, x_send, relay_send, g_recv,
    core_send, core_recv, s_send, s_recv,
):
    z_hi, x, core, y, z_lo = place()
    y_pair = y + 1 - 2 * (y % 2)
    at_y = device(z_hi, x, core, y_pair, z_lo)
    at_z = device(z_hi, x, core, y, 1 - z_lo)
    at_far = device(z_hi, x, core, 3 - y, z_lo)
    at_hi = device(1 - z_hi, x, core, y, z_lo)
    at_hi_far = device(1 - z_hi, x, core, 3 - y, z_lo)
    at_right = device(z_hi, (x + 1) % 4, core, y, z_lo)
    at_left = device(z_hi, (x + 3) % 4, core, y, z_lo)
    at_core = device(z_hi, x, 1 - core, y, z_lo)
    peers = (at_y, at_z, at_far, at_hi, at_hi_far, at_right, at_left, at_core)
    holder = y // 2 == z_hi
    chunk = acts.shape[0] // 4

    barrier = pltpu.get_barrier_semaphore()
    for peer in peers:
        pl.semaphore_signal(barrier, inc=1, device_id=peer, device_id_type=MESH)
    pl.semaphore_wait(barrier, len(peers))

    def remote(src, dst, send, recv, target):
        return pltpu.make_async_remote_copy(
            src_ref=src, dst_ref=dst, send_sem=send, recv_sem=recv, device_id=target, device_id_type=MESH
        )

    def arrived(ref, recv):
        remote(ref, ref, s_send, recv, at_core).wait_recv()

    own_h = pltpu.make_async_copy(acts, hbuf.at[0], local_sem.at[0])
    own_s = pltpu.make_async_copy(signs, sbuf.at[0], local_sem.at[1])
    own_g = pltpu.make_async_copy(grads, gbuf.at[0, core, 0], local_sem.at[2])
    to_hi = remote(grads, gbuf.at[0, core, 0], init_send.at[0], g_recv.at[0, 0], at_hi)
    to_far = remote(grads, gbuf.at[0, core, 1], init_send.at[0], g_recv.at[0, 1], at_far)
    to_hi_far = remote(grads, gbuf.at[0, core, 1], init_send.at[1], g_recv.at[0, 1], at_hi_far)

    @pl.when(holder)
    def _():
        own_g.start()
        to_hi.start()

    @pl.when(jnp.logical_not(holder))
    def _():
        to_far.start()
        to_hi_far.start()

    pending = []
    for first, second in zip((0, 1, 2, 3), (2, 3, 0, 1)):
        for num, slot, sends, target in ((first, 1, hy_send, at_y), (second, 2, hz_send, at_z)):
            copy = remote(
                acts.at[pl.ds(num * chunk, chunk)], hbuf.at[slot, pl.ds(num * chunk, chunk)],
                sends.at[num], h_recv.at[slot - 1, num], target,
            )
            copy.start()
            pending.append(copy)
    send_s = remote(signs, sbuf.at[1], s_send, s_recv, at_far)
    send_s.start()
    own_h.start()
    own_s.start()

    def rows(slot, num):
        return hbuf.at[slot, pl.ds(num * chunk, chunk)]

    def pass_on(slot, num):
        arrived(rows(slot, num), h_recv.at[slot - 1, num])
        sends, target = ((hz_send, at_z), (hy_send, at_y))[slot - 1]
        copy = remote(rows(slot, num), rows(3, num), sends.at[4 + num % 2], h_recv.at[2, num], target)
        copy.start()
        pending.append(copy)

    def to_sibling(slot, part):
        block = gbuf.at[slot, core, part]
        copy = remote(block, block, core_send.at[slot, part], core_recv.at[slot, part], at_core)
        copy.start()
        pending.append(copy)

    def spread(part):
        block = gbuf.at[0, core, part]
        for side, target in ((1, at_right), (2, at_left)):
            copy = remote(
                block, gbuf.at[side, core, part], x_send.at[side - 1, part], g_recv.at[side, part], target
            )
            copy.start()
            pending.append(copy)
        to_sibling(0, part)

    def around(part):
        for side in (1, 2):
            arrived(gbuf.at[side, core, part], g_recv.at[side, part])
        for side, target in ((1, at_right), (2, at_left)):

            @pl.when(core == side - 1)
            def _():
                remote(
                    gbuf.at[side, core, part], gbuf.at[3, core, part],
                    relay_send.at[part], g_recv.at[3, part], target,
                ).start()

        to_sibling(1, part)
        to_sibling(2, part)

    @pl.when(holder)
    def _():
        own_g.wait()

    @pl.when(jnp.logical_not(holder))
    def _():
        arrived(gbuf.at[0, core, 0], g_recv.at[0, 0])

    spread(0)
    pass_on(1, 0)
    pass_on(2, 2)
    arrived(gbuf.at[0, core, 1], g_recv.at[0, 1])
    spread(1)
    pass_on(1, 1)
    pass_on(2, 3)
    around(0)
    around(1)
    for part in range(2):
        arrived(gbuf.at[3, core, part], g_recv.at[3, part])
        to_sibling(3, part)

    total[...] = jnp.zeros_like(total)
    own_h.wait()
    for slot in range(4):
        for part in range(2):
            arrived(gbuf.at[slot, 1 - core, part], core_recv.at[slot, part])

    y_bit, depth = y % 2, acts.shape[0] // 2

    def step(num, carry):
        slot, half = num // 2, num % 2
        for at, which, nums in ((3, 1, (2, 3)), (4, 2, (0, 1)), (6, 3, (0, 1)), (7, 3, (2, 3))):

            @pl.when(num == at)
            def _():
                for one in nums:
                    arrived(rows(which, one), h_recv.at[which - 1, one])

        from_y, from_z = slot % 2, slot // 2
        tokens = ((y_bit + from_y) % 2) * 2 + (z_lo + from_z) % 2
        ahead = (tokens - x + 4) % 4
        source = (ahead + (ahead + 1) // 2) % 4
        left = hbuf[slot, pl.ds(pl.multiple_of(half * depth, depth), depth), :]
        for part in range(2):
            total[part] += lax.dot_general(
                left, gbuf[source, half, part], (((0,), (0,)), ((), ())), preferred_element_type=jnp.float32
            )
        return carry

    lax.fori_loop(0, 8, step, 0)
    own_s.wait()
    arrived(sbuf.at[1], s_recv)

    row_nums = lax.broadcasted_iota(jnp.int32, (BAND, BAND), 0)
    col_nums = lax.broadcasted_iota(jnp.int32, (BAND, BAND), 1)
    walsh = (1 - 2 * bit_parity(jnp.bitwise_and(row_nums, col_nums), 7)).astype(jnp.float32).astype(jnp.bfloat16)

    def mix(group, carry):
        band = pl.ds(pl.multiple_of(group * BAND, BAND), BAND)
        values = []
        for part in range(2):
            flipped = total[part, band, :] * sbuf[part, band, :].astype(jnp.float32)
            high = flipped.astype(jnp.bfloat16)
            low = (flipped - high.astype(jnp.float32)).astype(jnp.bfloat16)
            mixed = jnp.dot(walsh, high, preferred_element_type=jnp.float32)
            mixed = mixed + jnp.dot(walsh, low, preferred_element_type=jnp.float32)
            values += [mixed[:, k * LANES:(k + 1) * LANES] for k in range(4)]
        for stride in (1, 2, 4):
            values = [
                values[k - stride] - values[k] if k & stride else values[k] + values[k + stride]
                for k in range(8)
            ]
        for k in range(8):
            out[k, band, :] = values[k]
        return carry

    lax.fori_loop(0, total.shape[1] // BAND, mix, 0)

    for copy in pending:
        copy.wait_send()
    send_s.wait_send()
    for part in range(2):
        remote(
            gbuf.at[1, core, part], gbuf.at[3, core, part], relay_send.at[part], g_recv.at[3, part], at_core
        ).wait_send()
    to_hi.wait_send()

    @pl.when(jnp.logical_not(holder))
    def _():
        to_hi_far.wait_send()


def transform(hidden, out_grad, signs):
    tokens, units = hidden.shape
    part_tokens, features = out_grad.shape
    dma = pltpu.SemaphoreType.DMA
    return pl.pallas_call(
        transform_kernel,
        out_shape=jax.ShapeDtypeStruct((8, units, LANES), jnp.float32),
        in_specs=[pl.BlockSpec(memory_space=pl.ANY)] * 3,
        out_specs=pl.BlockSpec(memory_space=pltpu.VMEM),
        scratch_shapes=[
            pltpu.VMEM((4, tokens, units), jnp.bfloat16),
            pltpu.VMEM((4, 2, 2, part_tokens, features), jnp.bfloat16),
            pltpu.VMEM((2, units, features), jnp.bfloat16),
            pltpu.VMEM((2, units, features), jnp.float32),
            dma((3,)), dma((6,)), dma((6,)), dma((3, 4)), dma((2,)), dma((2, 2)), dma((2,)), dma((4, 2)),
            dma((4, 2)), dma((4, 2)), dma, dma,
        ],
        compiler_params=pltpu.CompilerParams(
            collective_id=0, has_side_effects=True, vmem_limit_bytes=48 * 1024 * 1024
        ),
        name="gather_transform",
    )(hidden, out_grad, signs)


def pick_kernel(spots, table, weights, out):
    lane_nums = lax.broadcasted_iota(jnp.int32, (8, LANES), 1)
    sub_nums = lax.broadcasted_iota(jnp.int32, (8, LANES), 0)
    unroll = 8

    for tile in range(8):

        def step(block, found):
            for inner in range(unroll):
                lane = block * unroll + inner
                rows = jnp.zeros((8, LANES), jnp.float32)
                for sub in range(8):
                    spot = spots[tile * 1024 + sub * LANES + lane]
                    row = jnp.broadcast_to(table[pl.ds(spot, 1), :], (8, LANES))
                    rows = row if sub == 0 else jnp.where(sub_nums == sub, row, rows)
                at = pl.multiple_of((tile * LANES + lane) * 8, 8)
                value = jnp.sum(rows * weights[pl.ds(at, 8), :], axis=1, keepdims=True)
                found = jnp.where(lane_nums == lane, value, found)
            return found

        found = lax.fori_loop(0, LANES // unroll, step, jnp.zeros((8, LANES), jnp.float32))
        out[2 * tile] = found[:4]
        out[2 * tile + 1] = found[4:]


def pick(spots, table, weights):
    return pl.pallas_call(
        pick_kernel,
        out_shape=jax.ShapeDtypeStruct((WIDE, 4, LANES), jnp.float32),
        in_specs=[
            pl.BlockSpec(memory_space=pltpu.SMEM),
            pl.BlockSpec(memory_space=pltpu.VMEM),
            pl.BlockSpec(memory_space=pltpu.VMEM),
        ],
        out_specs=pl.BlockSpec(memory_space=pltpu.VMEM),
        compiler_params=pltpu.CompilerParams(vmem_limit_bytes=32 * 1024 * 1024),
        name="pick",
    )(spots, table, weights)


def sum_kernel(terms, out, first, second, own, send1, recv1, send2, recv2, send3, recv3):
    wide, narrow = lax.axis_index("wide"), lax.axis_index("narrow")
    barrier = pltpu.get_barrier_semaphore()
    across = [(wide + d) % WIDE for d in range(1, WIDE)]
    along = [(narrow + d) % NARROW for d in range(1, NARROW)]
    for peer in across:
        pl.semaphore_signal(barrier, inc=1, device_id=(peer, narrow), device_id_type=MESH)
    for peer in along:
        pl.semaphore_signal(barrier, inc=1, device_id=(wide, peer), device_id_type=MESH)
    pl.semaphore_wait(barrier, WIDE + NARROW - 2)

    def remote(src, dst, send, recv, target):
        return pltpu.make_async_remote_copy(
            src_ref=src, dst_ref=dst, send_sem=send, recv_sem=recv, device_id=target, device_id_type=MESH
        )

    ones = [
        remote(terms.at[peer], first.at[d], send1.at[d], recv1.at[d], (peer, narrow))
        for d, peer in enumerate(across)
    ]
    for copy in ones:
        copy.start()
    value = terms[wide]
    for d, copy in enumerate(ones):
        copy.wait_recv()
        value = value + first[d]
    second[narrow] = value
    twos = [
        remote(second.at[narrow], second.at[narrow], send2.at[d], recv2.at[d], (wide, peer))
        for d, peer in enumerate(along)
    ]
    for copy in twos:
        copy.start()
    for d, copy in enumerate(twos):
        source = second.at[(narrow + NARROW - 1 - d) % NARROW]
        remote(source, source, send2.at[d], recv2.at[d], (wide, along[d])).wait_recv()
    for example in range(2):
        at = example * 4
        own[example] = (second[at] + second[at + 1]) + (second[at + 2] + second[at + 3])
    out[wide] = own[...]
    threes = [
        remote(own, out.at[wide], send3.at[d], recv3.at[d], (peer, narrow)) for d, peer in enumerate(across)
    ]
    for copy in threes:
        copy.start()
    for d, copy in enumerate(threes):
        source = out.at[(wide + WIDE - 1 - d) % WIDE]
        remote(own, source, send3.at[d], recv3.at[d], (across[d], narrow)).wait_recv()
    for copy in ones + twos + threes:
        copy.wait_send()


def sum_all(terms):
    dma = pltpu.SemaphoreType.DMA
    piece = terms.shape[1:]
    return pl.pallas_call(
        sum_kernel,
        out_shape=jax.ShapeDtypeStruct((WIDE, 2) + piece, jnp.float32),
        in_specs=[pl.BlockSpec(memory_space=pltpu.VMEM)],
        out_specs=pl.BlockSpec(memory_space=pltpu.VMEM),
        scratch_shapes=[
            pltpu.VMEM((WIDE - 1,) + piece, jnp.float32),
            pltpu.VMEM((NARROW,) + piece, jnp.float32),
            pltpu.VMEM((2,) + piece, jnp.float32),
            dma((WIDE - 1,)), dma((WIDE - 1,)), dma((NARROW - 1,)), dma((NARROW - 1,)),
            dma((WIDE - 1,)), dma((WIDE - 1,)),
        ],
        compiler_params=pltpu.CompilerParams(collective_id=1, has_side_effects=True),
        name="sum_all",
    )(terms)


def shards(hidden, out_grad, sign_bits, pick_rows, pick_cols):
    units, features = sign_bits.shape
    wide, narrow = lax.axis_index("wide"), lax.axis_index("narrow")
    signs = (2 * sign_bits - 1).astype(jnp.bfloat16)
    group, row = pick_rows // units, pick_rows % units
    block, col = pick_cols // features, pick_cols % features
    table_row = bit_parity(jnp.bitwise_and(block, 6), 3) * 4 + col // LANES
    spots = table_row * units + row
    sign = bit_parity(jnp.bitwise_and(group, wide), 4) + bit_parity(jnp.bitwise_and(block, narrow), 3)
    code = (col % LANES + LANES * jnp.bitwise_and(sign, 1)).reshape(8, 8, LANES).transpose(0, 2, 1).reshape(-1, 1)
    lanes = lax.broadcasted_iota(jnp.int32, (1, LANES), 1) + LANES
    scale = 1.0 / math.sqrt(float(SEQ) * SEQ * features * NARROW)
    weights = (1 - 2 * bit_parity(jnp.bitwise_and(code, lanes), 8)).astype(jnp.float32) * scale
    table = transform(hidden, out_grad, signs)
    terms = pick(spots, table.reshape(-1, LANES), weights)
    sums = sum_all(terms)
    return sums.reshape(WIDE, 2, -1).transpose(1, 0, 2).reshape(2, -1)


def solution(mesh):
    placed = (P("narrow", "wide"), P("wide", "narrow"), P("wide", "narrow"), P(), P())
    return jax.shard_map(shards, mesh=mesh, in_specs=placed, out_specs=P(), check_vma=False)
```

time: 495 us -> 99.2 us (0.20)
  waiting for transfers between devices: 353 us -> 0 us
  local copies, waits for them, and re-layouts: 99.9 us -> 2.59 us
  Pallas kernels: 0 us -> 89.5 us
  matrix products: 22.5 us -> 0 us
  between operations: 13.1 us -> 0.06 us
    all_gather x2 -> x0, waiting for transfers between devices: 206 us -> none  [the longest x1 148 us: shards(): acts_all = lax.all_gather(hidden, 'narrow', axis=0, tiled=True)]
    psum x1 -> x0, waiting for transfers between devices: 145 us -> none  [shards(): return lax.psum(terms, ('wide', 'narrow'))]
    gather x1 -> x0, local copies, waits for them, and re-layouts: 91.2 us -> none  [shards(): picked = local[:, position]]
    pallas_call x0 -> x3, Pallas kernels: none -> 89.5 us  [the longest x1 53 us: transform(): pl.pallas_call(transform_kernel, out_shape=jax.ShapeDtypeStruct((8, units...]
    dot_general x3 -> x0, matrix products: 22.5 us -> none  [the longest x1 9.82 us: shards(): jnp.einsum('esr,esc->erc', acts_all, grads_all, preferred_element_type=jn...]
    reshape x1, local copies, waits for them, and re-layouts: 7.22 us -> 1.52 us  [shards(): return sums.reshape(WIDE, 2, -1).transpose(1, 0, 2).reshape(2, -1)]
  transfers between devices with their start and end apart: 3 -> 0, of which waited for: 3 -> 0; matrix products, arithmetic and copies ran while one was open for 1% -> 0% of each run, Pallas kernels for 0% -> 0%
where the time goes in v2:
time: 99.2 us; the launch traced here: 98.9 us
  Pallas kernels  89.5 us (90%)
  other arithmetic  6.73 us (7%)
  local copies, waits for them, and re-layouts  2.59 us (3%)
    pallas_call x1, Pallas kernels, transform(): pl.pallas_call(transform_kernel, out_shape=jax.ShapeDtypeStruct((8, units...  53 us
    pallas_call x1, Pallas kernels, sum_all(): pl.pallas_call(sum_kernel, out_shape=jax.ShapeDtypeStruct((WIDE, 2) + pie...  19.8 us
    pallas_call x1, Pallas kernels, pick(): pl.pallas_call(pick_kernel, out_shape=jax.ShapeDtypeStruct((WIDE, 4, LANE...  16.7 us
    mul x1, other arithmetic, shards(): (1 - 2 * bit_parity(jnp.bitwise_and(code, lanes), 8)).astype(jnp.float32)  3.96 us

profile of v2, /device:TPU:1, one launch (start us, length us, event | category | flops | bytes accessed | tf_op | source)
XLA Modules:
  0.0 98.9 jit_solution(5992040692152661028)
XLA Ops:
  0.0 0.0 copy-start.1
  0.0 0.0 copy-start
  0.0 1.0 %fusion.24 = (s32[8,128,8]{1,2,0:T(8,128)S(1)}, s32[8192]{0:T(1024)S(1)}) fusion(s32[8192]{0:T(1024)} %param.8, s32[]{:T(128)S(6)} %axis_index.25, s32[]{:T(128)S(6)} %axis_index.23, s32[8192]{0:T(1024)} %param.9), kind=kLoop, calls=%fused_computation.45 | loop fusion | flops 745472 | bytes 131080 | tf_op jit(solution)/shard_map/transpose | solution.py:375
  1.0 0.2 copy.8
  1.2 0.3 and.154
  1.5 1.8 %add_convert_fusion.signs = bf16[896,512]{1,0:T(8,128)(2,1)S(1)} fusion(s32[896,512]{1,0:T(8,128)} %param.7), kind=kLoop, calls=%fused_computation.28 | loop fusion | flops 1376256 | bytes 2752512 | tf_op jit(solution)/shard_map/convert_element_type | solution.py:369
  3.2 0.0 copy-done.1
  3.2 0.0 copy-done
  3.3 53.0 %gather_transform.1 = f32[8,896,128]{2,1,0:T(8,128)S(1)} custom-call(bf16[512,896]{1,0:T(8,128)(2,1)S(1)} %copy-done, bf16[256,512]{1,0:T(8,128)(2,1)S(1)} %copy-done.1, bf16[896,512]{1,0:T(8,128)(2,1)S(1)} %add_convert_fusion.signs), custom_call_target="tpu_custom_call" | custom-call | tf_op jit(solution)/shard_map/gather_transform/pallas_call | solution.py:234
  56.2 4.0 %fusion.12.weights = f32[8192,128]{1,0:T(8,128)S(1)} fusion(s32[128]{0:T(128)S(1)} %iota_add_fusion, s32[8192]{0:T(1024)S(1)} %and.154), kind=kLoop, calls=%fused_computation.20 | loop fusion | flops 30408704 | bytes 4227584 | tf_op jit(solution)/shard_map/mul | solution.py:378
  60.2 16.7 %pick.1.terms = f32[16,4,128]{2,1,0:T(4,128)S(1)} custom-call(s32[8192]{0:T(1024)S(1)} %get-tuple-element.6.spots, f32[7168,128]{1,0:T(8,128)S(1)} %bitcast.8, f32[8192,128]{1,0:T(8,128)S(1)} %fusion.12.weights), custom_call_target="tpu_custom_call" | custom-call | tf_op jit(solution)/shard_map/pick/pallas_call | solution.py:280
  76.9 0.0 copy-start.2
  76.9 0.6 copy-done.2
  77.5 19.8 %sum_all.1 = f32[16,2,4,128]{3,2,1,0:T(4,128)} custom-call(f32[16,4,128]{2,1,0:T(4,128)} %copy-done.2), custom_call_target="tpu_custom_call" | custom-call | tf_op jit(solution)/shard_map/sum_all/pallas_call | solution.py:349
  97.4 1.5 %reshape.21 = f32[16,2,512]{2,1,0:T(2,128)} reshape(f32[16,2,4,128]{3,2,1,0:T(4,128)} %sum_all.1) | data formatting | bytes 131072 | tf_op jit(solution)/shard_map/reshape | solution.py:382
  (1 shorter events, 0.0 us)
Async XLA Ops:
  0.0 3.2 %copy-start.1 = (bf16[256,512]{1,0:T(8,128)(2,1)S(1)}, bf16[256,512]{1,0:T(8,128)(2,1)}, u32[]{:S(2)}) copy-start(bf16[256,512]{1,0:T(8,128)(2,1)} %grads.1) | copy-start | bytes 786436
  0.0 3.2 %copy-start = (bf16[512,896]{1,0:T(8,128)(2,1)S(1)}, bf16[512,896]{1,0:T(8,128)(2,1)}, u32[]{:S(2)}) copy-start(bf16[512,896]{1,0:T(8,128)(2,1)} %acts.1) | copy-start | bytes 2752516
  76.9 0.6 copy-start.2

commit v3 on v2

v3 whole, which is shorter than its diff:
```python
import math

import jax
import jax.numpy as jnp
from jax import lax
from jax.experimental import pallas as pl
from jax.experimental.pallas import tpu as pltpu
from jax.sharding import PartitionSpec as P

SEQ = 2048
BAND = 128
LANES = 128
PIECES = 8
SPREAD = 16
BY_Z = (0,)
MESH = pl.DeviceIdType.MESH


def bit_parity(value, count):
    total = jnp.zeros_like(value)
    for bit_num in range(count):
        total = total + jnp.bitwise_and(jnp.right_shift(value, bit_num), 1)
    return jnp.bitwise_and(total, 1)


def place():
    wide, narrow = lax.axis_index("wide"), lax.axis_index("narrow")
    return wide // 8, (wide // 2) % 4, wide % 2, narrow // 2, narrow % 2


def device(z_hi, x, core, y, z_lo):
    return (z_hi * 8 + x * 2 + core, y * 2 + z_lo)


def sketch_kernel(
    acts, grads, sign_bits, pick_rows, pick_cols, out,
    hbuf, gbuf, sraw, sbuf, total, table, spots, codes, weights, spots_smem, terms, first, second, own,
    local_sem, spot_sem, hy_send, hz_send, h_recv, init_send, x_send, relay_send, g_recv,
    core_send, core_recv, s_send, s_recv, send1, recv1, send2, recv2, send3, recv3,
):
    wide, narrow = lax.axis_index("wide"), lax.axis_index("narrow")
    z_hi, x, core, y, z_lo = place()
    units = sraw.shape[0]
    y_pair = y + 1 - 2 * (y % 2)
    at_y = device(z_hi, x, core, y_pair, z_lo)
    at_z = device(z_hi, x, core, y, 1 - z_lo)
    at_far = device(z_hi, x, core, 3 - y, z_lo)
    at_hi = device(1 - z_hi, x, core, y, z_lo)
    at_hi_far = device(1 - z_hi, x, core, 3 - y, z_lo)
    at_right = device(z_hi, (x + 1) % 4, core, y, z_lo)
    at_left = device(z_hi, (x + 3) % 4, core, y, z_lo)
    at_core = device(z_hi, x, 1 - core, y, z_lo)
    holder = y // 2 == z_hi
    chunk = acts.shape[0] // 4

    piece = x * 2 + core
    member = (z_hi * 4 + y) * 2 + z_lo
    pieces = [(piece + d) % PIECES for d in range(1, PIECES)]
    members = [(member + d) % SPREAD for d in range(1, SPREAD)]
    across = [device(z_hi, t // 2, t % 2, y, z_lo) for t in pieces]
    along = [device(g // 8, x, core, (g // 2) % 4, g % 2) for g in members]

    barrier = pltpu.get_barrier_semaphore()
    for peer in across + along:
        pl.semaphore_signal(barrier, inc=1, device_id=peer, device_id_type=MESH)
    bits_in = pltpu.make_async_copy(sign_bits, sraw, local_sem.at[1])
    bits_in.start()
    own_h = pltpu.make_async_copy(acts, hbuf.at[0], local_sem.at[0])
    own_h.start()
    pl.semaphore_wait(barrier, len(across + along))

    def remote(src, dst, send, recv, target):
        return pltpu.make_async_remote_copy(
            src_ref=src, dst_ref=dst, send_sem=send, recv_sem=recv, device_id=target, device_id_type=MESH
        )

    def arrived(ref, recv):
        remote(ref, ref, s_send, recv, at_core).wait_recv()

    own_g = pltpu.make_async_copy(grads, gbuf.at[0, core, 0], local_sem.at[2])
    to_hi = remote(grads, gbuf.at[0, core, 0], init_send.at[0], g_recv.at[0, 0], at_hi)
    to_far = remote(grads, gbuf.at[0, core, 1], init_send.at[0], g_recv.at[0, 1], at_far)
    to_hi_far = remote(grads, gbuf.at[0, core, 1], init_send.at[1], g_recv.at[0, 1], at_hi_far)

    @pl.when(holder)
    def _():
        own_g.start()
        to_hi.start()

    @pl.when(jnp.logical_not(holder))
    def _():
        to_far.start()
        to_hi_far.start()

    pending = []
    by_y = tuple(num for num in range(4) if num not in BY_Z)
    for first_num, second_num in zip(BY_Z + by_y, by_y + BY_Z):
        for num, slot, sends, target in ((first_num, 1, hy_send, at_y), (second_num, 2, hz_send, at_z)):
            copy = remote(
                acts.at[pl.ds(num * chunk, chunk)], hbuf.at[slot, pl.ds(num * chunk, chunk)],
                sends.at[num], h_recv.at[slot - 1, num], target,
            )
            copy.start()
            pending.append(copy)

    def rows(slot, num):
        return hbuf.at[slot, pl.ds(num * chunk, chunk)]

    def pass_on(slot, num):
        arrived(rows(slot, num), h_recv.at[slot - 1, num])
        sends, target = ((hz_send, at_z), (hy_send, at_y))[slot - 1]
        copy = remote(rows(slot, num), rows(3, num), sends.at[4 + num], h_recv.at[2, num], target)
        copy.start()
        pending.append(copy)

    def to_sibling(slot, part):
        block = gbuf.at[slot, core, part]
        copy = remote(block, block, core_send.at[slot, part], core_recv.at[slot, part], at_core)
        copy.start()
        pending.append(copy)

    def spread(part):
        block = gbuf.at[0, core, part]
        for side, target in ((1, at_right), (2, at_left)):
            copy = remote(
                block, gbuf.at[side, core, part], x_send.at[side - 1, part], g_recv.at[side, part], target
            )
            copy.start()
            pending.append(copy)
        to_sibling(0, part)

    def around(part):
        for side in (1, 2):
            arrived(gbuf.at[side, core, part], g_recv.at[side, part])
        for side, target in ((1, at_right), (2, at_left)):

            @pl.when(core == side - 1)
            def _():
                remote(
                    gbuf.at[side, core, part], gbuf.at[3, core, part],
                    relay_send.at[part], g_recv.at[3, part], target,
                ).start()

        to_sibling(1, part)
        to_sibling(2, part)

    bits_in.wait()

    def to_sign(group, carry):
        band = pl.ds(pl.multiple_of(group * BAND, BAND), BAND)
        sbuf[0, band, :] = (2 * sraw[band, :] - 1).astype(jnp.float32).astype(jnp.bfloat16)
        return carry

    lax.fori_loop(0, units // BAND, to_sign, 0)

    sampled, features = pick_rows[...], pick_cols[...]
    group = jnp.zeros_like(sampled)
    for num in range(1, 16):
        group = group + (sampled >= num * units).astype(jnp.int32)
    block, col = features // 512, features % 512
    upper = bit_parity(jnp.bitwise_and(block, 6), 3)
    spot = (upper * 4 + col // LANES) * units + sampled - group * units
    ahead_of = (lax.broadcasted_iota(jnp.int32, (8, LANES), 1) // 16 + 8 - lax.broadcasted_iota(jnp.int32, (8, LANES), 0)) % 8
    for tile in range(PIECES):
        straight = spot[tile * 8:(tile + 1) * 8]
        turned = straight
        for d in range(1, 8):
            turned = jnp.where(ahead_of == d, pltpu.roll(pltpu.roll(straight, 8 - d, 0), 16 * d, 1), turned)
        for part in range(4):
            spots[tile * 4 + part] = turned[2 * part:2 * part + 2]
    sign = bit_parity(jnp.bitwise_and(group, wide), 4) + bit_parity(jnp.bitwise_and(block, narrow), 3)
    codes[...] = col % LANES + LANES * (sign % 2)

    lane_bits = lax.broadcasted_iota(jnp.int32, (8, LANES), 1) + LANES

    def weigh(first_tile, last_tile):
        def some(num, code):
            for inner in range(16):
                odd = jnp.bitwise_and(jnp.broadcast_to(code[:, inner:inner + 1], (8, LANES)), lane_bits)
                odd = jnp.bitwise_and(lax.population_count(odd), 1)
                weights[num // 8, num % 8 * 16 + inner] = jnp.where(odd == 1, -1.0, 1.0).astype(jnp.float32)
            code = pltpu.roll(code, LANES - 16, 1)
            after = jnp.minimum(num // 8 + 1, PIECES - 1)
            return jnp.where(num % 8 == 7, codes[pl.ds(pl.multiple_of(after * 8, 8), 8), :], code)

        lax.fori_loop(first_tile * 8, last_tile * 8, some, codes[first_tile * 8:(first_tile + 1) * 8, :])

    def spots_part(d, part):
        tile = lax.rem(piece + 1 + d, PIECES)
        return pltpu.make_async_copy(spots.at[tile * 4 + part], spots_smem.at[part], spot_sem.at[part])

    @pl.when(holder)
    def _():
        own_g.wait()

    @pl.when(jnp.logical_not(holder))
    def _():
        arrived(gbuf.at[0, core, 0], g_recv.at[0, 0])

    spread(0)
    send_s = remote(sbuf.at[0], sbuf.at[1], s_send, s_recv, at_far)
    send_s.start()
    weigh(0, 2)
    pass_on(1, BY_Z[0])
    pass_on(2, by_y[0])
    weigh(2, 4)
    arrived(gbuf.at[0, core, 1], g_recv.at[0, 1])
    spread(1)
    for num in BY_Z[1:]:
        pass_on(1, num)
    pass_on(2, by_y[1])
    weigh(4, 6)
    around(0)
    weigh(6, 8)
    for num in by_y[2:]:
        pass_on(2, num)
    around(1)
    for part in range(2):
        arrived(gbuf.at[3, core, part], g_recv.at[3, part])
        to_sibling(3, part)

    total[...] = jnp.zeros_like(total)
    own_h.wait()
    for slot in range(4):
        for part in range(2):
            arrived(gbuf.at[slot, 1 - core, part], core_recv.at[slot, part])

    y_bit, depth = y % 2, acts.shape[0] // 2

    def step(num, carry):
        slot, half = num // 2, num % 2
        for which in (1, 2, 3):
            for one in range(4):
                if not ((which == 1 and one in BY_Z) or (which == 2 and one in by_y)):

                    @pl.when(num == 2 * which + one // 2)
                    def _():
                        arrived(rows(which, one), h_recv.at[which - 1, one])

        from_y, from_z = slot % 2, slot // 2
        tokens = ((y_bit + from_y) % 2) * 2 + (z_lo + from_z) % 2
        ahead = (tokens - x + 4) % 4
        source = (ahead + (ahead + 1) // 2) % 4
        left = hbuf[slot, pl.ds(pl.multiple_of(half * depth, depth), depth), :]
        for part in range(2):
            total[part] += lax.dot_general(
                left, gbuf[source, half, part], (((0,), (0,)), ((), ())), preferred_element_type=jnp.float32
            )
        return carry

    for part in range(4):
        spots_part(0, part).start()
    lax.fori_loop(0, 8, step, 0)
    arrived(sbuf.at[1], s_recv)

    row_nums = lax.broadcasted_iota(jnp.int32, (BAND, 2 * BAND), 0)
    col_nums = lax.broadcasted_iota(jnp.int32, (BAND, 2 * BAND), 1)
    walsh = (1 - 2 * bit_parity(jnp.bitwise_and(row_nums, col_nums), 7)).astype(jnp.float32).astype(jnp.bfloat16)

    def mix(group, carry):
        band = pl.ds(pl.multiple_of(group * BAND, BAND), BAND)
        values = []
        for part in range(2):
            flipped = total[part, band, :] * sbuf[part, band, :].astype(jnp.float32)
            high = flipped.astype(jnp.bfloat16)
            low = (flipped - high.astype(jnp.float32)).astype(jnp.bfloat16)
            both = jnp.concatenate([high, low], axis=0)
            mixed = jnp.dot(walsh, both, preferred_element_type=jnp.float32)
            values += [mixed[:, k * LANES:(k + 1) * LANES] for k in range(4)]
        for stride in (1, 2, 4):
            values = [
                values[k - stride] - values[k] if k & stride else values[k] + values[k + stride]
                for k in range(8)
            ]
        for k in range(8):
            table[pl.ds(pl.multiple_of(k * units + group * BAND, BAND), BAND), :] = values[k]
        return carry

    lax.fori_loop(0, units // BAND, mix, 0)

    lane_nums = lax.broadcasted_iota(jnp.int32, (8, LANES), 1)
    sub_nums = lax.broadcasted_iota(jnp.int32, (8, LANES), 0)

    def pick(d, carry):
        tile = lax.rem(piece + 1 + d, PIECES)
        found = jnp.zeros((8, LANES), jnp.float32)
        for part in range(4):
            spots_part(d, part).wait()
            for num in (2 * part, 2 * part + 1):
                for inner in range(16):
                    for sub in range(8):
                        spot = spots_smem[part, num % 2, sub * 16 + inner]
                        row = jnp.broadcast_to(table[pl.ds(spot, 1), :], (8, LANES))
                        taken = row if sub == 0 else jnp.where(sub_nums == sub, row, taken)
                    lane = num * 16 + inner
                    value = jnp.sum(taken * weights[tile, lane], axis=1, keepdims=True)
                    found = jnp.where(lane_nums == lane, value, found)

            @pl.when(d < PIECES - 1)
            def _():
                spots_part(d + 1, part).start()

        for num in range(1, PIECES):

            @pl.when(d == num)
            def _():
                ones[num - 1].start()

        terms[d] = found
        return carry

    ones = [
        remote(terms.at[d], first.at[d], send1.at[d], recv1.at[d], across[d]) for d in range(PIECES - 1)
    ]
    lax.fori_loop(0, PIECES, pick, 0)
    value = terms[PIECES - 1]
    for d, copy in enumerate(ones):
        copy.wait_recv()
        value = value + first[d]
    second[member] = value
    twos = [
        remote(second.at[member], second.at[member], send2.at[d], recv2.at[d], along[d]) for d in range(SPREAD - 1)
    ]
    for copy in twos:
        copy.start()
    for d in range(SPREAD - 1):
        source = second.at[(member + SPREAD - 1 - d) % SPREAD]
        remote(source, source, send2.at[d], recv2.at[d], along[d]).wait_recv()
    scale = 1.0 / math.sqrt(float(SEQ) * SEQ * 4096)
    for example in range(2):
        parts = [second[8 * hi + 4 * example + num] for hi in range(2) for num in range(4)]
        while len(parts) > 1:
            parts = [parts[k] + parts[k + 1] for k in range(0, len(parts), 2)]
        own[example] = parts[0] * scale
    out[piece] = own[...]
    threes = [
        remote(own, out.at[piece], send3.at[d], recv3.at[d], across[d]) for d in range(PIECES - 1)
    ]
    for copy in threes:
        copy.start()
    for d in range(PIECES - 1):
        source = out.at[(piece + PIECES - 1 - d) % PIECES]
        remote(own, source, send3.at[d], recv3.at[d], across[d]).wait_recv()

    for copy in pending + ones + twos + threes:
        copy.wait_send()
    send_s.wait_send()
    for part in range(2):
        remote(
            gbuf.at[1, core, part], gbuf.at[3, core, part], relay_send.at[part], g_recv.at[3, part], at_core
        ).wait_send()
    to_hi.wait_send()

    @pl.when(jnp.logical_not(holder))
    def _():
        to_hi_far.wait_send()


def shards(hidden, out_grad, sign_bits, pick_rows, pick_cols):
    units, features = sign_bits.shape
    tokens = hidden.shape[0]
    part_tokens = out_grad.shape[0]
    dma = pltpu.SemaphoreType.DMA
    tile = (8, LANES)
    hbm, vmem = pl.BlockSpec(memory_space=pltpu.HBM), pl.BlockSpec(memory_space=pltpu.VMEM)
    sums = pl.pallas_call(
        sketch_kernel,
        out_shape=jax.ShapeDtypeStruct((PIECES, 2) + tile, jnp.float32),
        in_specs=[hbm, hbm, hbm, vmem, vmem],
        out_specs=vmem,
        scratch_shapes=[
            pltpu.VMEM((4, tokens, units), jnp.bfloat16),
            pltpu.VMEM((4, 2, 2, part_tokens, features), jnp.bfloat16),
            pltpu.VMEM((units, features), jnp.int32),
            pltpu.VMEM((2, units, features), jnp.bfloat16),
            pltpu.VMEM((2, units, features), jnp.float32),
            pltpu.VMEM((8 * units, LANES), jnp.float32),
            pltpu.VMEM((PIECES * 4, 2, LANES), jnp.int32),
            pltpu.VMEM((PIECES * 8, LANES), jnp.int32),
            pltpu.VMEM((PIECES, LANES) + tile, jnp.float32),
            pltpu.SMEM((4, 2, LANES), jnp.int32),
            pltpu.VMEM((PIECES,) + tile, jnp.float32),
            pltpu.VMEM((PIECES - 1,) + tile, jnp.float32),
            pltpu.VMEM((SPREAD,) + tile, jnp.float32),
            pltpu.VMEM((2,) + tile, jnp.float32),
            dma((3,)), dma((4,)), dma((8,)), dma((8,)), dma((3, 4)), dma((2,)), dma((2, 2)), dma((2,)), dma((4, 2)),
            dma((4, 2)), dma((4, 2)), dma, dma,
            dma((PIECES - 1,)), dma((PIECES - 1,)), dma((SPREAD - 1,)), dma((SPREAD - 1,)),
            dma((PIECES - 1,)), dma((PIECES - 1,)),
        ],
        compiler_params=pltpu.CompilerParams(
            collective_id=0, has_side_effects=True, vmem_limit_bytes=62 * 1024 * 1024
        ),
        name="sketch",
    )(hidden, out_grad, sign_bits, pick_rows.reshape(-1, LANES), pick_cols.reshape(-1, LANES))
    return sums.transpose(1, 0, 2, 3).reshape(2, -1)


def solution(mesh):
    placed = (P("narrow", "wide"), P("wide", "narrow"), P("wide", "narrow"), P(), P())
    return jax.shard_map(shards, mesh=mesh, in_specs=placed, out_specs=P(), check_vma=False)
```

time: 99.2 us -> 72.4 us (0.73)
  Pallas kernels: 89.5 us -> 70.6 us
  other arithmetic: 6.73 us -> 0 us
  local copies, waits for them, and re-layouts: 2.59 us -> 1.53 us
    pallas_call x3 -> x1, Pallas kernels: 89.5 us -> 70.6 us  [shards(): pl.pallas_call(sketch_kernel, out_shape=jax.ShapeDtypeStruct((PIECES, 2)...]
    mul x1 -> x0, other arithmetic: 3.96 us -> none  [shards(): (1 - 2 * bit_parity(jnp.bitwise_and(code, lanes), 8)).astype(jnp.float32)]
    convert_element_type x1 -> x0, other arithmetic: 1.75 us -> none  [shards(): signs = (2 * sign_bits - 1).astype(jnp.bfloat16)]
    reshape x1 -> x0, local copies, waits for them, and re-layouts: 1.52 us -> none  [shards(): return sums.reshape(WIDE, 2, -1).transpose(1, 0, 2).reshape(2, -1)]
    transpose x1 -> x0, other arithmetic: 1.01 us -> none  [shards(): (col % LANES + LANES * jnp.bitwise_and(sign, 1)).reshape(8, 8, LANES)]
where the time goes in v3:
time: 72.4 us; the launch traced here: 72.2 us
  Pallas kernels  70.6 us (98%)
  local copies, waits for them, and re-layouts  1.53 us (2%)
    pallas_call x1, Pallas kernels, shards(): pl.pallas_call(sketch_kernel, out_shape=jax.ShapeDtypeStruct((PIECES, 2)...  70.6 us
    unnamed x2, local copies, waits for them, and re-layouts  1.53 us

profile of v3, /device:TPU:1, one launch (start us, length us, event | category | flops | bytes accessed | tf_op | source)
XLA Modules:
  0.0 72.2 jit_solution(2871682867666867855)
XLA Ops:
  0.0 70.6 %sketch.1 = f32[8,2,8,128]{3,2,1,0:T(8,128)} custom-call(bf16[512,896]{1,0:T(8,128)(2,1)} %acts.1, bf16[256,512]{1,0:T(8,128)(2,1)} %grads.1, s32[896,512]{1,0:T(8,128)} %sign_bits.1, s32[64,128]{1,0:T(8,128)} %bitcast.11, s32[64,128]{1,0:T(8,128)} %bitcast.12), custom_call_target="tpu_custom_call" | custom-call | tf_op jit(solution)/shard_map/sketch/pallas_call | solution.py:366
  70.6 0.8 %copy_bitcast_fusion.1 = f32[1,2,64,128]{3,2,1,0:T(8,128)S(1)} fusion(f32[8,2,8,128]{3,2,1,0:T(8,128)} %sketch.1), kind=kLoop, calls=%fused_computation.1 | loop fusion | bytes 131072
  71.5 0.7 copy.10

commit v4 on v3

--- a/solution.py
+++ b/solution.py
@@ -12,7 +12,8 @@
 LANES = 128
 PIECES = 8
 SPREAD = 16
-BY_Z = (0,)
+CHUNKS = 8
+BY_Z = (0, 1)
 MESH = pl.DeviceIdType.MESH
 
 
@@ -23,9 +24,17 @@
     return jnp.bitwise_and(total, 1)
 
 
+def div(value, by):
+    return lax.div(value, jnp.int32(by))
+
+
+def mod(value, by):
+    return lax.rem(value, jnp.int32(by))
+
+
 def place():
     wide, narrow = lax.axis_index("wide"), lax.axis_index("narrow")
-    return wide // 8, (wide // 2) % 4, wide % 2, narrow // 2, narrow % 2
+    return div(wide, 8), mod(div(wide, 2), 4), mod(wide, 2), div(narrow, 2), mod(narrow, 2)
 
 
 def device(z_hi, x, core, y, z_lo):
@@ -34,31 +43,32 @@
 
 def sketch_kernel(
     acts, grads, sign_bits, pick_rows, pick_cols, out,
-    hbuf, gbuf, sraw, sbuf, total, table, spots, codes, weights, spots_smem, terms, first, second, own,
+    picks, hbuf, gbuf, sraw, sbuf, total, table, spots, codes, weights, spots_smem, terms, first, second, own,
     local_sem, spot_sem, hy_send, hz_send, h_recv, init_send, x_send, relay_send, g_recv,
     core_send, core_recv, s_send, s_recv, send1, recv1, send2, recv2, send3, recv3,
 ):
     wide, narrow = lax.axis_index("wide"), lax.axis_index("narrow")
     z_hi, x, core, y, z_lo = place()
     units = sraw.shape[0]
-    y_pair = y + 1 - 2 * (y % 2)
+    y_bit, upper_y = mod(y, 2), div(y, 2)
+    y_pair = y + 1 - 2 * y_bit
     at_y = device(z_hi, x, core, y_pair, z_lo)
     at_z = device(z_hi, x, core, y, 1 - z_lo)
     at_far = device(z_hi, x, core, 3 - y, z_lo)
     at_hi = device(1 - z_hi, x, core, y, z_lo)
     at_hi_far = device(1 - z_hi, x, core, 3 - y, z_lo)
-    at_right = device(z_hi, (x + 1) % 4, core, y, z_lo)
-    at_left = device(z_hi, (x + 3) % 4, core, y, z_lo)
+    at_right = device(z_hi, mod(x + 1, 4), core, y, z_lo)
+    at_left = device(z_hi, mod(x + 3, 4), core, y, z_lo)
     at_core = device(z_hi, x, 1 - core, y, z_lo)
-    holder = y // 2 == z_hi
-    chunk = acts.shape[0] // 4
+    holder = upper_y == z_hi
+    chunk = acts.shape[0] // CHUNKS
 
     piece = x * 2 + core
     member = (z_hi * 4 + y) * 2 + z_lo
-    pieces = [(piece + d) % PIECES for d in range(1, PIECES)]
-    members = [(member + d) % SPREAD for d in range(1, SPREAD)]
-    across = [device(z_hi, t // 2, t % 2, y, z_lo) for t in pieces]
-    along = [device(g // 8, x, core, (g // 2) % 4, g % 2) for g in members]
+    pieces = [mod(piece + d, PIECES) for d in range(1, PIECES)]
+    members = [mod(member + d, SPREAD) for d in range(1, SPREAD)]
+    across = [(z_hi * 8 + t, narrow) for t in pieces]
+    along = [(div(g, 8) * 8 + piece, mod(g, 8)) for g in members]
 
     barrier = pltpu.get_barrier_semaphore()
     for peer in across + along:
@@ -67,6 +77,12 @@
     bits_in.start()
     own_h = pltpu.make_async_copy(acts, hbuf.at[0], local_sem.at[0])
     own_h.start()
+    picks_in = [
+        pltpu.make_async_copy(source, picks.at[num], local_sem.at[3 + num])
+        for num, source in enumerate((pick_rows, pick_cols))
+    ]
+    for copy in picks_in:
+        copy.start()
     pl.semaphore_wait(barrier, len(across + along))
 
     def remote(src, dst, send, recv, target):
@@ -93,7 +109,7 @@
         to_hi_far.start()
 
     pending = []
-    by_y = tuple(num for num in range(4) if num not in BY_Z)
+    by_y = tuple(num for num in range(CHUNKS) if num not in BY_Z)
     for first_num, second_num in zip(BY_Z + by_y, by_y + BY_Z):
         for num, slot, sends, target in ((first_num, 1, hy_send, at_y), (second_num, 2, hz_send, at_z)):
             copy = remote(
@@ -109,7 +125,7 @@
     def pass_on(slot, num):
         arrived(rows(slot, num), h_recv.at[slot - 1, num])
         sends, target = ((hz_send, at_z), (hy_send, at_y))[slot - 1]
-        copy = remote(rows(slot, num), rows(3, num), sends.at[4 + num], h_recv.at[2, num], target)
+        copy = remote(rows(slot, num), rows(3, num), sends.at[CHUNKS + num], h_recv.at[2, num], target)
         copy.start()
         pending.append(copy)
 
@@ -153,7 +169,10 @@
 
     lax.fori_loop(0, units // BAND, to_sign, 0)
 
-    sampled, features = pick_rows[...], pick_cols[...]
+    send_s = remote(sbuf.at[0], sbuf.at[1], s_send, s_recv, at_far)
+    for copy in picks_in:
+        copy.wait()
+    sampled, features = picks[0], picks[1]
     group = jnp.zeros_like(sampled)
     for num in range(1, 16):
         group = group + (sampled >= num * units).astype(jnp.int32)
@@ -189,6 +208,8 @@
         tile = lax.rem(piece + 1 + d, PIECES)
         return pltpu.make_async_copy(spots.at[tile * 4 + part], spots_smem.at[part], spot_sem.at[part])
 
+    send_s.start()
+
     @pl.when(holder)
     def _():
         own_g.wait()
@@ -197,27 +218,35 @@
     def _():
         arrived(gbuf.at[0, core, 0], g_recv.at[0, 0])
 
+    def half_of(nums, which):
+        middle = (len(nums) + 1) // 2
+        return nums[:middle] if which == 0 else nums[middle:]
+
     spread(0)
-    send_s = remote(sbuf.at[0], sbuf.at[1], s_send, s_recv, at_far)
-    send_s.start()
-    weigh(0, 2)
-    pass_on(1, BY_Z[0])
-    pass_on(2, by_y[0])
-    weigh(2, 4)
+    weigh(0, 3)
     arrived(gbuf.at[0, core, 1], g_recv.at[0, 1])
     spread(1)
-    for num in BY_Z[1:]:
+    weigh(3, 6)
+    for num in half_of(BY_Z, 0):
         pass_on(1, num)
-    pass_on(2, by_y[1])
-    weigh(4, 6)
     around(0)
     weigh(6, 8)
-    for num in by_y[2:]:
+    early, late = half_of(by_y, 0), half_of(by_y, 1)
+    for num in half_of(early, 0):
         pass_on(2, num)
+    for num in half_of(BY_Z, 1):
+        pass_on(1, num)
     around(1)
-    for part in range(2):
-        arrived(gbuf.at[3, core, part], g_recv.at[3, part])
-        to_sibling(3, part)
+    for num in half_of(early, 1):
+        pass_on(2, num)
+    arrived(gbuf.at[3, core, 0], g_recv.at[3, 0])
+    to_sibling(3, 0)
+    for num in half_of(late, 0):
+        pass_on(2, num)
+    arrived(gbuf.at[3, core, 1], g_recv.at[3, 1])
+    to_sibling(3, 1)
+    for num in half_of(late, 1):
+        pass_on(2, num)
 
     total[...] = jnp.zeros_like(total)
     own_h.wait()
@@ -225,22 +254,22 @@
         for part in range(2):
             arrived(gbuf.at[slot, 1 - core, part], core_recv.at[slot, part])
 
-    y_bit, depth = y % 2, acts.shape[0] // 2
+    depth = acts.shape[0] // 2
 
     def step(num, carry):
-        slot, half = num // 2, num % 2
+        slot, half = div(num, 2), mod(num, 2)
         for which in (1, 2, 3):
-            for one in range(4):
+            for one in range(CHUNKS):
                 if not ((which == 1 and one in BY_Z) or (which == 2 and one in by_y)):
 
-                    @pl.when(num == 2 * which + one // 2)
+                    @pl.when(num == 2 * which + one // (CHUNKS // 2))
                     def _():
                         arrived(rows(which, one), h_recv.at[which - 1, one])
 
-        from_y, from_z = slot % 2, slot // 2
-        tokens = ((y_bit + from_y) % 2) * 2 + (z_lo + from_z) % 2
-        ahead = (tokens - x + 4) % 4
-        source = (ahead + (ahead + 1) // 2) % 4
+        from_y, from_z = mod(slot, 2), div(slot, 2)
+        tokens = mod(y_bit + from_y, 2) * 2 + mod(z_lo + from_z, 2)
+        ahead = mod(tokens - x + 4, 4)
+        source = mod(ahead + div(ahead + 1, 2), 4)
         left = hbuf[slot, pl.ds(pl.multiple_of(half * depth, depth), depth), :]
         for part in range(2):
             total[part] += lax.dot_general(
@@ -300,11 +329,12 @@
             def _():
                 spots_part(d + 1, part).start()
 
-        for num in range(1, PIECES):
-
-            @pl.when(d == num)
-            def _():
-                ones[num - 1].start()
+            if part == 0:
+                for num in range(1, PIECES):
+
+                    @pl.when(d == num)
+                    def _():
+                        ones[num - 1].start()
 
         terms[d] = found
         return carry
@@ -324,7 +354,7 @@
     for copy in twos:
         copy.start()
     for d in range(SPREAD - 1):
-        source = second.at[(member + SPREAD - 1 - d) % SPREAD]
+        source = second.at[mod(member + SPREAD - 1 - d, SPREAD)]
         remote(source, source, send2.at[d], recv2.at[d], along[d]).wait_recv()
     scale = 1.0 / math.sqrt(float(SEQ) * SEQ * 4096)
     for example in range(2):
@@ -332,14 +362,15 @@
         while len(parts) > 1:
             parts = [parts[k] + parts[k + 1] for k in range(0, len(parts), 2)]
         own[example] = parts[0] * scale
-    out[piece] = own[...]
+    for example in range(2):
+        out[example, piece] = own[example]
     threes = [
-        remote(own, out.at[piece], send3.at[d], recv3.at[d], across[d]) for d in range(PIECES - 1)
+        remote(own, out.at[:, piece], send3.at[d], recv3.at[d], across[d]) for d in range(PIECES - 1)
     ]
     for copy in threes:
         copy.start()
     for d in range(PIECES - 1):
-        source = out.at[(piece + PIECES - 1 - d) % PIECES]
+        source = out.at[:, mod(piece + PIECES - 1 - d, PIECES)]
         remote(own, source, send3.at[d], recv3.at[d], across[d]).wait_recv()
 
     for copy in pending + ones + twos + threes:
@@ -365,10 +396,11 @@
     hbm, vmem = pl.BlockSpec(memory_space=pltpu.HBM), pl.BlockSpec(memory_space=pltpu.VMEM)
     sums = pl.pallas_call(
         sketch_kernel,
-        out_shape=jax.ShapeDtypeStruct((PIECES, 2) + tile, jnp.float32),
-        in_specs=[hbm, hbm, hbm, vmem, vmem],
+        out_shape=jax.ShapeDtypeStruct((2, PIECES) + tile, jnp.float32),
+        in_specs=[hbm] * 5,
         out_specs=vmem,
         scratch_shapes=[
+            pltpu.VMEM((2, PIECES * 8, LANES), jnp.int32),
             pltpu.VMEM((4, tokens, units), jnp.bfloat16),
             pltpu.VMEM((4, 2, 2, part_tokens, features), jnp.bfloat16),
             pltpu.VMEM((units, features), jnp.int32),
@@ -383,7 +415,7 @@
             pltpu.VMEM((PIECES - 1,) + tile, jnp.float32),
             pltpu.VMEM((SPREAD,) + tile, jnp.float32),
             pltpu.VMEM((2,) + tile, jnp.float32),
-            dma((3,)), dma((4,)), dma((8,)), dma((8,)), dma((3, 4)), dma((2,)), dma((2, 2)), dma((2,)), dma((4, 2)),
+            dma((5,)), dma((4,)), dma((2 * CHUNKS,)), dma((2 * CHUNKS,)), dma((3, CHUNKS)), dma((2,)), dma((2, 2)), dma((2,)), dma((4, 2)),
             dma((4, 2)), dma((4, 2)), dma, dma,
             dma((PIECES - 1,)), dma((PIECES - 1,)), dma((SPREAD - 1,)), dma((SPREAD - 1,)),
             dma((PIECES - 1,)), dma((PIECES - 1,)),
@@ -393,7 +425,7 @@
         ),
         name="sketch",
     )(hidden, out_grad, sign_bits, pick_rows.reshape(-1, LANES), pick_cols.reshape(-1, LANES))
-    return sums.transpose(1, 0, 2, 3).reshape(2, -1)
+    return sums.reshape(2, -1)
 
 
 def solution(mesh):

time: 72.4 us -> 71 us (0.981)
  Pallas kernels: 70.6 us -> 69.3 us
    pallas_call x1, Pallas kernels: 70.6 us -> 69.3 us  [shards(): pl.pallas_call(sketch_kernel, out_shape=jax.ShapeDtypeStruct((2, PIECES)...]
    unnamed x2 -> x1, local copies, waits for them, and re-layouts: 1.53 us -> 1.52 us
where the time goes in v4:
time: 71 us; the launch traced here: 70.8 us
  Pallas kernels  69.3 us (98%)
  local copies, waits for them, and re-layouts  1.52 us (2%)
    pallas_call x1, Pallas kernels, shards(): pl.pallas_call(sketch_kernel, out_shape=jax.ShapeDtypeStruct((2, PIECES)...  69.3 us
    unnamed x1, local copies, waits for them, and re-layouts  1.52 us

profile of v4, /device:TPU:1, one launch (start us, length us, event | category | flops | bytes accessed | tf_op | source)
XLA Modules:
  0.0 70.8 jit_solution(1297006597341454437)
XLA Ops:
  0.0 69.3 %sketch.1 = f32[2,8,8,128]{3,2,1,0:T(8,128)} custom-call(bf16[512,896]{1,0:T(8,128)(2,1)} %acts.1, bf16[256,512]{1,0:T(8,128)(2,1)} %grads.1, s32[896,512]{1,0:T(8,128)} %sign_bits.1, s32[64,128]{1,0:T(8,128)} %bitcast.8, s32[64,128]{1,0:T(8,128)} %bitcast.9), custom_call_target="tpu_custom_call" | custom-call | tf_op jit(solution)/shard_map/sketch/pallas_call | solution.py:397
  69.3 1.5 %copy.8 = f32[1,2,64,128]{3,1,2,0:T(2,128)} copy(f32[1,2,64,128]{3,2,1,0:T(8,128)} %bitcast.7) | data formatting | bytes 131072

commit v5 on v4

--- a/solution.py
+++ b/solution.py
@@ -12,8 +12,10 @@
 LANES = 128
 PIECES = 8
 SPREAD = 16
+UNITS = 4
 CHUNKS = 8
-BY_Z = (0, 1)
+BY_Z = (0, 1, 2)
+LEAD = 2
 MESH = pl.DeviceIdType.MESH
 
 
@@ -43,8 +45,8 @@
 
 def sketch_kernel(
     acts, grads, sign_bits, pick_rows, pick_cols, out,
-    picks, hbuf, gbuf, sraw, sbuf, total, table, spots, codes, weights, spots_smem, terms, first, second, own,
-    local_sem, spot_sem, hy_send, hz_send, h_recv, init_send, x_send, relay_send, g_recv,
+    picks, hbuf, gbuf, transit, sraw, sbuf, total, table, spots, codes, weights, spots_smem, terms, first, second, own,
+    local_sem, spot_sem, hy_send, hz_send, h_recv, init_send, far_send, t_send, t_recv, x_send, relay_send, g_recv,
     core_send, core_recv, s_send, s_recv, send1, recv1, send2, recv2, send3, recv3,
 ):
     wide, narrow = lax.axis_index("wide"), lax.axis_index("narrow")
@@ -55,8 +57,7 @@
     at_y = device(z_hi, x, core, y_pair, z_lo)
     at_z = device(z_hi, x, core, y, 1 - z_lo)
     at_far = device(z_hi, x, core, 3 - y, z_lo)
-    at_hi = device(1 - z_hi, x, core, y, z_lo)
-    at_hi_far = device(1 - z_hi, x, core, 3 - y, z_lo)
+    at_cross = device(1 - z_hi, x, core, y, 1 - z_lo)
     at_right = device(z_hi, mod(x + 1, 4), core, y, z_lo)
     at_left = device(z_hi, mod(x + 3, 4), core, y, z_lo)
     at_core = device(z_hi, x, 1 - core, y, z_lo)
@@ -94,30 +95,65 @@
         remote(ref, ref, s_send, recv, at_core).wait_recv()
 
     own_g = pltpu.make_async_copy(grads, gbuf.at[0, core, 0], local_sem.at[2])
-    to_hi = remote(grads, gbuf.at[0, core, 0], init_send.at[0], g_recv.at[0, 0], at_hi)
-    to_far = remote(grads, gbuf.at[0, core, 1], init_send.at[0], g_recv.at[0, 1], at_far)
-    to_hi_far = remote(grads, gbuf.at[0, core, 1], init_send.at[1], g_recv.at[0, 1], at_hi_far)
+    few = grads.shape[0] // 2
+
+    def piece_of(ref, unit):
+        return ref.at[pl.ds(unit % 2 * few, few)]
+
+    def unit_at(slot, half, unit):
+        return gbuf.at[slot, half, unit // 2, pl.ds(unit % 2 * few, few)]
+
+    follower = jnp.logical_not(holder)
+    cross = [
+        remote(piece_of(grads, unit), transit.at[unit], init_send.at[unit], t_recv.at[unit], at_cross)
+        for unit in range(2)
+    ]
+    to_far = [
+        remote(piece_of(grads, unit), unit_at(0, core, 2 + unit), far_send.at[unit], g_recv.at[0, 2 + unit], at_far)
+        for unit in range(2)
+    ]
+    hand_on = [
+        remote(transit.at[unit], unit_at(0, core, unit), t_send.at[unit], g_recv.at[0, unit], at_z)
+        for unit in range(2)
+    ]
+    hand_over = [
+        remote(transit.at[unit], transit.at[2 + unit], t_send.at[unit], t_recv.at[2 + unit], at_z)
+        for unit in range(2)
+    ]
+    onward = [
+        remote(
+            transit.at[2 + unit], unit_at(0, core, 2 + unit), far_send.at[unit], g_recv.at[0, 2 + unit], at_far
+        )
+        for unit in range(2)
+    ]
+    for copy in cross:
+        copy.start()
 
     @pl.when(holder)
     def _():
         own_g.start()
-        to_hi.start()
-
-    @pl.when(jnp.logical_not(holder))
-    def _():
-        to_far.start()
-        to_hi_far.start()
+
+    @pl.when(follower)
+    def _():
+        for copy in to_far:
+            copy.start()
 
     pending = []
     by_y = tuple(num for num in range(CHUNKS) if num not in BY_Z)
-    for first_num, second_num in zip(BY_Z + by_y, by_y + BY_Z):
-        for num, slot, sends, target in ((first_num, 1, hy_send, at_y), (second_num, 2, hz_send, at_z)):
-            copy = remote(
-                acts.at[pl.ds(num * chunk, chunk)], hbuf.at[slot, pl.ds(num * chunk, chunk)],
-                sends.at[num], h_recv.at[slot - 1, num], target,
-            )
-            copy.start()
-            pending.append(copy)
+    def activations(slot, num):
+        sends, target = ((hy_send, at_y), (hz_send, at_z))[slot - 1]
+        copy = remote(
+            acts.at[pl.ds(num * chunk, chunk)], hbuf.at[slot, pl.ds(num * chunk, chunk)],
+            sends.at[num], h_recv.at[slot - 1, num], target,
+        )
+        pending.append(copy)
+        return copy
+
+    by_z_pair = [activations(2, num) for num in by_y + BY_Z]
+    for copy in by_z_pair[:LEAD]:
+        copy.start()
+    for num in BY_Z + by_y:
+        activations(1, num).start()
 
     def rows(slot, num):
         return hbuf.at[slot, pl.ds(num * chunk, chunk)]
@@ -129,36 +165,67 @@
         copy.start()
         pending.append(copy)
 
-    def to_sibling(slot, part):
-        block = gbuf.at[slot, core, part]
-        copy = remote(block, block, core_send.at[slot, part], core_recv.at[slot, part], at_core)
-        copy.start()
+    def to_sibling(slot, unit):
+        block = unit_at(slot, core, unit)
+        copy = remote(block, block, core_send.at[slot, unit], core_recv.at[slot, unit], at_core)
         pending.append(copy)
-
-    def spread(part):
-        block = gbuf.at[0, core, part]
-        for side, target in ((1, at_right), (2, at_left)):
-            copy = remote(
-                block, gbuf.at[side, core, part], x_send.at[side - 1, part], g_recv.at[side, part], target
+        return copy
+
+    spreads = [
+        [
+            remote(
+                unit_at(0, core, unit), unit_at(side, core, unit), x_send.at[side - 1, unit],
+                g_recv.at[side, unit], target,
             )
+            for side, target in ((1, at_right), (2, at_left))
+        ]
+        for unit in range(UNITS)
+    ]
+    for copies in spreads:
+        pending.extend(copies)
+    own_siblings = [to_sibling(0, unit) for unit in range(UNITS)]
+
+    def spread(unit):
+        for copy in spreads[unit]:
             copy.start()
-            pending.append(copy)
-        to_sibling(0, part)
-
-    def around(part):
+        own_siblings[unit].start()
+
+    def around(unit):
         for side in (1, 2):
-            arrived(gbuf.at[side, core, part], g_recv.at[side, part])
+            arrived(unit_at(side, core, unit), g_recv.at[side, unit])
         for side, target in ((1, at_right), (2, at_left)):
 
             @pl.when(core == side - 1)
             def _():
                 remote(
-                    gbuf.at[side, core, part], gbuf.at[3, core, part],
-                    relay_send.at[part], g_recv.at[3, part], target,
+                    unit_at(side, core, unit), unit_at(3, core, unit),
+                    relay_send.at[unit], g_recv.at[3, unit], target,
                 ).start()
 
-        to_sibling(1, part)
-        to_sibling(2, part)
+        to_sibling(1, unit).start()
+        to_sibling(2, unit).start()
+
+    def opposite(unit):
+        arrived(unit_at(3, core, unit), g_recv.at[3, unit])
+        to_sibling(3, unit).start()
+
+    def transfer(unit):
+        arrived(transit.at[unit], t_recv.at[unit])
+
+        @pl.when(holder)
+        def _():
+            hand_over[unit].start()
+
+        @pl.when(follower)
+        def _():
+            hand_on[unit].start()
+
+    def move_on(unit):
+        arrived(transit.at[2 + unit], t_recv.at[2 + unit])
+        onward[unit].start()
+
+    def own_arrived(unit):
+        arrived(unit_at(0, core, unit), g_recv.at[0, unit])
 
     bits_in.wait()
 
@@ -208,51 +275,83 @@
         tile = lax.rem(piece + 1 + d, PIECES)
         return pltpu.make_async_copy(spots.at[tile * 4 + part], spots_smem.at[part], spot_sem.at[part])
 
+
+    @pl.when(holder)
+    def _():
+        own_g.wait()
+        spread(0)
+        spread(1)
+
+    transfer(0)
+
+    @pl.when(holder)
+    def _():
+        own_arrived(2)
+        spread(2)
+
+    weigh(0, 1)
+    transfer(1)
+    for copy in by_z_pair[LEAD:]:
+        copy.start()
+
+    @pl.when(holder)
+    def _():
+        own_arrived(3)
+        spread(3)
+        move_on(0)
+
+    @pl.when(follower)
+    def _():
+        own_arrived(0)
+        spread(0)
+
+    for num in BY_Z:
+        pass_on(1, num)
+    weigh(1, 2)
+
+    @pl.when(holder)
+    def _():
+        move_on(1)
+
+    @pl.when(follower)
+    def _():
+        own_arrived(1)
+        spread(1)
+        own_arrived(2)
+        spread(2)
+
     send_s.start()
-
-    @pl.when(holder)
-    def _():
-        own_g.wait()
-
-    @pl.when(jnp.logical_not(holder))
-    def _():
-        arrived(gbuf.at[0, core, 0], g_recv.at[0, 0])
-
-    def half_of(nums, which):
-        middle = (len(nums) + 1) // 2
-        return nums[:middle] if which == 0 else nums[middle:]
-
-    spread(0)
-    weigh(0, 3)
-    arrived(gbuf.at[0, core, 1], g_recv.at[0, 1])
-    spread(1)
-    weigh(3, 6)
-    for num in half_of(BY_Z, 0):
-        pass_on(1, num)
     around(0)
+    weigh(2, 3)
+
+    @pl.when(follower)
+    def _():
+        own_arrived(3)
+        spread(3)
+
+    around(1)
+    weigh(3, 5)
+    opposite(0)
+    third = (len(by_y) + 2) // 3
+    for num in by_y[:third]:
+        pass_on(2, num)
+    around(2)
+    weigh(5, 6)
+    opposite(1)
+    around(3)
     weigh(6, 8)
-    early, late = half_of(by_y, 0), half_of(by_y, 1)
-    for num in half_of(early, 0):
+    for num in by_y[third:2 * third]:
         pass_on(2, num)
-    for num in half_of(BY_Z, 1):
-        pass_on(1, num)
-    around(1)
-    for num in half_of(early, 1):
-        pass_on(2, num)
-    arrived(gbuf.at[3, core, 0], g_recv.at[3, 0])
-    to_sibling(3, 0)
-    for num in half_of(late, 0):
-        pass_on(2, num)
-    arrived(gbuf.at[3, core, 1], g_recv.at[3, 1])
-    to_sibling(3, 1)
-    for num in half_of(late, 1):
+    opposite(2)
+    opposite(3)
+    for num in by_y[2 * third:]:
         pass_on(2, num)
 
     total[...] = jnp.zeros_like(total)
     own_h.wait()
     for slot in range(4):
-        for part in range(2):
-            arrived(gbuf.at[slot, 1 - core, part], core_recv.at[slot, part])
+        for unit in range(UNITS):
+            arrived(unit_at(slot, 1 - core, unit), core_recv.at[slot, unit])
 
     depth = acts.shape[0] // 2
 
@@ -376,15 +475,13 @@
     for copy in pending + ones + twos + threes:
         copy.wait_send()
     send_s.wait_send()
-    for part in range(2):
+    for unit in range(UNITS):
         remote(
-            gbuf.at[1, core, part], gbuf.at[3, core, part], relay_send.at[part], g_recv.at[3, part], at_core
+            unit_at(1, core, unit), unit_at(3, core, unit), relay_send.at[unit], g_recv.at[3, unit], at_core
         ).wait_send()
-    to_hi.wait_send()
-
-    @pl.when(jnp.logical_not(holder))
-    def _():
-        to_hi_far.wait_send()
+
+    for copy in cross + to_far + hand_on:
+        copy.wait_send()
 
 
 def shards(hidden, out_grad, sign_bits, pick_rows, pick_cols):
@@ -403,6 +500,7 @@
             pltpu.VMEM((2, PIECES * 8, LANES), jnp.int32),
             pltpu.VMEM((4, tokens, units), jnp.bfloat16),
             pltpu.VMEM((4, 2, 2, part_tokens, features), jnp.bfloat16),
+            pltpu.VMEM((UNITS, part_tokens // 2, features), jnp.bfloat16),
             pltpu.VMEM((units, features), jnp.int32),
             pltpu.VMEM((2, units, features), jnp.bfloat16),
             pltpu.VMEM((2, units, features), jnp.float32),
@@ -415,8 +513,8 @@
             pltpu.VMEM((PIECES - 1,) + tile, jnp.float32),
             pltpu.VMEM((SPREAD,) + tile, jnp.float32),
             pltpu.VMEM((2,) + tile, jnp.float32),
-            dma((5,)), dma((4,)), dma((2 * CHUNKS,)), dma((2 * CHUNKS,)), dma((3, CHUNKS)), dma((2,)), dma((2, 2)), dma((2,)), dma((4, 2)),
-            dma((4, 2)), dma((4, 2)), dma, dma,
+            dma((5,)), dma((4,)), dma((2 * CHUNKS,)), dma((2 * CHUNKS,)), dma((3, CHUNKS)), dma((2,)), dma((2,)), dma((2,)), dma((UNITS,)), dma((2, UNITS)),
+            dma((UNITS,)), dma((4, UNITS)), dma((4, UNITS)), dma((4, UNITS)), dma, dma,
             dma((PIECES - 1,)), dma((PIECES - 1,)), dma((SPREAD - 1,)), dma((SPREAD - 1,)),
             dma((PIECES - 1,)), dma((PIECES - 1,)),
         ],

time: 71 us -> 68.7 us (0.968)
  Pallas kernels: 69.3 us -> 67 us
    pallas_call x1, Pallas kernels: 69.3 us -> 67 us  [shards(): pl.pallas_call(sketch_kernel, out_shape=jax.ShapeDtypeStruct((2, PIECES)...]
where the time goes in v5:
time: 68.7 us; the launch traced here: 68.6 us
  Pallas kernels  67 us (98%)
  local copies, waits for them, and re-layouts  1.52 us (2%)
    pallas_call x1, Pallas kernels, shards(): pl.pallas_call(sketch_kernel, out_shape=jax.ShapeDtypeStruct((2, PIECES)...  67 us
    unnamed x1, local copies, waits for them, and re-layouts  1.52 us

profile of v5, /device:TPU:1, one launch (start us, length us, event | category | flops | bytes accessed | tf_op | source)
XLA Modules:
  0.0 68.6 jit_solution(4741635799800678873)
XLA Ops:
  0.0 67.0 %sketch.1 = f32[2,8,8,128]{3,2,1,0:T(8,128)} custom-call(bf16[512,896]{1,0:T(8,128)(2,1)} %acts.1, bf16[256,512]{1,0:T(8,128)(2,1)} %grads.1, s32[896,512]{1,0:T(8,128)} %sign_bits.1, s32[64,128]{1,0:T(8,128)} %bitcast.8, s32[64,128]{1,0:T(8,128)} %bitcast.9), custom_call_target="tpu_custom_call" | custom-call | tf_op jit(solution)/shard_map/sketch/pallas_call | solution.py:494
  67.0 1.5 %copy.8 = f32[1,2,64,128]{3,1,2,0:T(2,128)} copy(f32[1,2,64,128]{3,2,1,0:T(8,128)} %bitcast.7) | data formatting | bytes 131072

commit v6 on v5

--- a/solution.py
+++ b/solution.py
@@ -14,7 +14,7 @@
 SPREAD = 16
 UNITS = 4
 CHUNKS = 8
-BY_Z = (0, 1, 2)
+BY_Z = (5, 6, 7)
 LEAD = 2
 MESH = pl.DeviceIdType.MESH
 
@@ -66,7 +66,9 @@
 
     piece = x * 2 + core
     member = (z_hi * 4 + y) * 2 + z_lo
-    pieces = [mod(piece + d, PIECES) for d in range(1, PIECES)]
+    ways = ((2, 0), (2, 1), (1, 0), (1, 1), (3, 0), (3, 1), (0, 1))
+    pieces = [mod(x + dx, 4) * 2 + mod(core + dc, 2) for dx, dc in ways]
+    sources = [mod(x + 4 - dx, 4) * 2 + mod(core + dc, 2) for dx, dc in ways]
     members = [mod(member + d, SPREAD) for d in range(1, SPREAD)]
     across = [(z_hi * 8 + t, narrow) for t in pieces]
     along = [(div(g, 8) * 8 + piece, mod(g, 8)) for g in members]
@@ -252,8 +254,8 @@
         turned = straight
         for d in range(1, 8):
             turned = jnp.where(ahead_of == d, pltpu.roll(pltpu.roll(straight, 8 - d, 0), 16 * d, 1), turned)
-        for part in range(4):
-            spots[tile * 4 + part] = turned[2 * part:2 * part + 2]
+        for part in range(2):
+            spots[tile * 2 + part] = turned[4 * part:4 * part + 4]
     sign = bit_parity(jnp.bitwise_and(group, wide), 4) + bit_parity(jnp.bitwise_and(block, narrow), 3)
     codes[...] = col % LANES + LANES * (sign % 2)
 
@@ -271,9 +273,14 @@
 
         lax.fori_loop(first_tile * 8, last_tile * 8, some, codes[first_tile * 8:(first_tile + 1) * 8, :])
 
-    def spots_part(d, part):
-        tile = lax.rem(piece + 1 + d, PIECES)
-        return pltpu.make_async_copy(spots.at[tile * 4 + part], spots_smem.at[part], spot_sem.at[part])
+    def turn(d):
+        pair = div(d, 2)
+        ahead = 2 + 3 * pair + 3 * div(pair, 2) + 2 * div(pair, 3)
+        return mod(x + ahead, 4) * 2 + mod(core + d + div(d, 6), 2)
+
+    def spots_part(d, part, buffer):
+        tile = turn(d)
+        return pltpu.make_async_copy(spots.at[tile * 2 + part], spots_smem.at[2 * buffer + part], spot_sem.at[2 * buffer + part])
 
 
     @pl.when(holder)
@@ -376,8 +383,9 @@
             )
         return carry
 
-    for part in range(4):
-        spots_part(0, part).start()
+    for part in range(2):
+        spots_part(0, part, 0).start()
+        spots_part(1, part, 1).start()
     lax.fori_loop(0, 8, step, 0)
     arrived(sbuf.at[1], s_recv)
 
@@ -389,10 +397,10 @@
         band = pl.ds(pl.multiple_of(group * BAND, BAND), BAND)
         values = []
         for part in range(2):
-            flipped = total[part, band, :] * sbuf[part, band, :].astype(jnp.float32)
-            high = flipped.astype(jnp.bfloat16)
-            low = (flipped - high.astype(jnp.float32)).astype(jnp.bfloat16)
-            both = jnp.concatenate([high, low], axis=0)
+            value, flip = total[part, band, :], sbuf[part, band, :]
+            high = value.astype(jnp.bfloat16)
+            low = (value - high.astype(jnp.float32)).astype(jnp.bfloat16)
+            both = jnp.concatenate([high * flip, low * flip], axis=0)
             mixed = jnp.dot(walsh, both, preferred_element_type=jnp.float32)
             values += [mixed[:, k * LANES:(k + 1) * LANES] for k in range(4)]
         for stride in (1, 2, 4):
@@ -409,24 +417,24 @@
     lane_nums = lax.broadcasted_iota(jnp.int32, (8, LANES), 1)
     sub_nums = lax.broadcasted_iota(jnp.int32, (8, LANES), 0)
 
-    def pick(d, carry):
-        tile = lax.rem(piece + 1 + d, PIECES)
+    def pick(d, buffer):
+        tile = turn(d)
         found = jnp.zeros((8, LANES), jnp.float32)
-        for part in range(4):
-            spots_part(d, part).wait()
-            for num in (2 * part, 2 * part + 1):
+        for part in range(2):
+            spots_part(d, part, buffer).wait()
+            for num in range(4 * part, 4 * part + 4):
                 for inner in range(16):
                     for sub in range(8):
-                        spot = spots_smem[part, num % 2, sub * 16 + inner]
+                        spot = spots_smem[2 * buffer + part, num % 4, sub * 16 + inner]
                         row = jnp.broadcast_to(table[pl.ds(spot, 1), :], (8, LANES))
                         taken = row if sub == 0 else jnp.where(sub_nums == sub, row, taken)
                     lane = num * 16 + inner
                     value = jnp.sum(taken * weights[tile, lane], axis=1, keepdims=True)
                     found = jnp.where(lane_nums == lane, value, found)
 
-            @pl.when(d < PIECES - 1)
+            @pl.when(d < PIECES - 2)
             def _():
-                spots_part(d + 1, part).start()
+                spots_part(d + 2, part, buffer).start()
 
             if part == 0:
                 for num in range(1, PIECES):
@@ -436,12 +444,16 @@
                         ones[num - 1].start()
 
         terms[d] = found
+
+    def pick_two(num, carry):
+        pick(2 * num, 0)
+        pick(2 * num + 1, 1)
         return carry
 
     ones = [
         remote(terms.at[d], first.at[d], send1.at[d], recv1.at[d], across[d]) for d in range(PIECES - 1)
     ]
-    lax.fori_loop(0, PIECES, pick, 0)
+    lax.fori_loop(0, PIECES // 2, pick_two, 0)
     value = terms[PIECES - 1]
     for d, copy in enumerate(ones):
         copy.wait_recv()
@@ -452,6 +464,16 @@
     ]
     for copy in twos:
         copy.start()
+    for copy in pending:
+        copy.wait_send()
+    send_s.wait_send()
+    for unit in range(UNITS):
+        remote(
+            unit_at(1, core, unit), unit_at(3, core, unit), relay_send.at[unit], g_recv.at[3, unit], at_core
+        ).wait_send()
+
+    for copy in cross + to_far + hand_on:
+        copy.wait_send()
     for d in range(SPREAD - 1):
         source = second.at[mod(member + SPREAD - 1 - d, SPREAD)]
         remote(source, source, send2.at[d], recv2.at[d], along[d]).wait_recv()
@@ -469,18 +491,10 @@
     for copy in threes:
         copy.start()
     for d in range(PIECES - 1):
-        source = out.at[:, mod(piece + PIECES - 1 - d, PIECES)]
+        source = out.at[:, sources[d]]
         remote(own, source, send3.at[d], recv3.at[d], across[d]).wait_recv()
 
-    for copy in pending + ones + twos + threes:
-        copy.wait_send()
-    send_s.wait_send()
-    for unit in range(UNITS):
-        remote(
-            unit_at(1, core, unit), unit_at(3, core, unit), relay_send.at[unit], g_recv.at[3, unit], at_core
-        ).wait_send()
-
-    for copy in cross + to_far + hand_on:
+    for copy in ones + twos + threes:
         copy.wait_send()
 
 
@@ -505,10 +519,10 @@
             pltpu.VMEM((2, units, features), jnp.bfloat16),
             pltpu.VMEM((2, units, features), jnp.float32),
             pltpu.VMEM((8 * units, LANES), jnp.float32),
-            pltpu.VMEM((PIECES * 4, 2, LANES), jnp.int32),
+            pltpu.VMEM((PIECES * 2, 4, LANES), jnp.int32),
             pltpu.VMEM((PIECES * 8, LANES), jnp.int32),
             pltpu.VMEM((PIECES, LANES) + tile, jnp.float32),
-            pltpu.SMEM((4, 2, LANES), jnp.int32),
+            pltpu.SMEM((4, 4, LANES), jnp.int32),
             pltpu.VMEM((PIECES,) + tile, jnp.float32),
             pltpu.VMEM((PIECES - 1,) + tile, jnp.float32),
             pltpu.VMEM((SPREAD,) + tile, jnp.float32),

time: 68.7 us -> 66.9 us (0.974)
  Pallas kernels: 67 us -> 65.2 us
    pallas_call x1, Pallas kernels: 67 us -> 65.2 us  [shards(): pl.pallas_call(sketch_kernel, out_shape=jax.ShapeDtypeStruct((2, PIECES)...]
where the time goes in v6:
time: 66.9 us; the launch traced here: 66.8 us
  Pallas kernels  65.2 us (97%)
  local copies, waits for them, and re-layouts  1.52 us (2%)
    pallas_call x1, Pallas kernels, shards(): pl.pallas_call(sketch_kernel, out_shape=jax.ShapeDtypeStruct((2, PIECES)...  65.2 us
    unnamed x1, local copies, waits for them, and re-layouts  1.52 us

profile of v6, /device:TPU:1, one launch (start us, length us, event | category | flops | bytes accessed | tf_op | source)
XLA Modules:
  0.0 66.8 jit_solution(13307154336423830928)
XLA Ops:
  0.0 65.2 %sketch.1 = f32[2,8,8,128]{3,2,1,0:T(8,128)} custom-call(bf16[512,896]{1,0:T(8,128)(2,1)} %acts.1, bf16[256,512]{1,0:T(8,128)(2,1)} %grads.1, s32[896,512]{1,0:T(8,128)} %sign_bits.1, s32[64,128]{1,0:T(8,128)} %bitcast.8, s32[64,128]{1,0:T(8,128)} %bitcast.9), custom_call_target="tpu_custom_call" | custom-call | tf_op jit(solution)/shard_map/sketch/pallas_call | solution.py:508
  65.2 1.5 %copy.8 = f32[1,2,64,128]{3,1,2,0:T(2,128)} copy(f32[1,2,64,128]{3,2,1,0:T(8,128)} %bitcast.7) | data formatting | bytes 131072

commit v7 on v6

--- a/solution.py
+++ b/solution.py
@@ -412,7 +412,7 @@
             table[pl.ds(pl.multiple_of(k * units + group * BAND, BAND), BAND), :] = values[k]
         return carry
 
-    lax.fori_loop(0, units // BAND, mix, 0)
+    lax.fori_loop(0, units // BAND, mix, 0, unroll=True)
 
     lane_nums = lax.broadcasted_iota(jnp.int32, (8, LANES), 1)
     sub_nums = lax.broadcasted_iota(jnp.int32, (8, LANES), 0)

time: 66.9 us -> 66.3 us (level)
  no operation moved by 1% of the time
where the time goes in v7:
time: 66.3 us; the launch traced here: 66.1 us
  Pallas kernels  64.6 us (97%)
  local copies, waits for them, and re-layouts  1.52 us (2%)
    pallas_call x1, Pallas kernels, shards(): pl.pallas_call(sketch_kernel, out_shape=jax.ShapeDtypeStruct((2, PIECES)...  64.6 us
    unnamed x1, local copies, waits for them, and re-layouts  1.52 us

profile of v7, /device:TPU:1, one launch (start us, length us, event | category | flops | bytes accessed | tf_op | source)
XLA Modules:
  0.0 66.1 jit_solution(293017931939858590)
XLA Ops:
  0.0 64.6 %sketch.1 = f32[2,8,8,128]{3,2,1,0:T(8,128)} custom-call(bf16[512,896]{1,0:T(8,128)(2,1)} %acts.1, bf16[256,512]{1,0:T(8,128)(2,1)} %grads.1, s32[896,512]{1,0:T(8,128)} %sign_bits.1, s32[64,128]{1,0:T(8,128)} %bitcast.8, s32[64,128]{1,0:T(8,128)} %bitcast.9), custom_call_target="tpu_custom_call" | custom-call | tf_op jit(solution)/shard_map/sketch/pallas_call | solution.py:508
  64.6 1.5 %copy.8 = f32[1,2,64,128]{3,1,2,0:T(2,128)} copy(f32[1,2,64,128]{3,2,1,0:T(8,128)} %bitcast.7) | data formatting | bytes 131072

commit v8 on v7

--- a/solution.py
+++ b/solution.py
@@ -386,7 +386,7 @@
     for part in range(2):
         spots_part(0, part, 0).start()
         spots_part(1, part, 1).start()
-    lax.fori_loop(0, 8, step, 0)
+    lax.fori_loop(0, 8, step, 0, unroll=2)
     arrived(sbuf.at[1], s_recv)
 
     row_nums = lax.broadcasted_iota(jnp.int32, (BAND, 2 * BAND), 0)

time: 66.3 us -> 66.3 us (level)
  no operation moved by 1% of the time
where the time goes in v8:
time: 66.3 us; the launch traced here: 66.1 us
  Pallas kernels  64.6 us (97%)
  local copies, waits for them, and re-layouts  1.52 us (2%)
    pallas_call x1, Pallas kernels, shards(): pl.pallas_call(sketch_kernel, out_shape=jax.ShapeDtypeStruct((2, PIECES)...  64.6 us
    unnamed x1, local copies, waits for them, and re-layouts  1.52 us

profile of v8, /device:TPU:1, one launch (start us, length us, event | category | flops | bytes accessed | tf_op | source)
XLA Modules:
  0.0 66.1 jit_solution(453587947250034709)
XLA Ops:
  0.0 64.6 %sketch.1 = f32[2,8,8,128]{3,2,1,0:T(8,128)} custom-call(bf16[512,896]{1,0:T(8,128)(2,1)} %acts.1, bf16[256,512]{1,0:T(8,128)(2,1)} %grads.1, s32[896,512]{1,0:T(8,128)} %sign_bits.1, s32[64,128]{1,0:T(8,128)} %bitcast.8, s32[64,128]{1,0:T(8,128)} %bitcast.9), custom_call_target="tpu_custom_call" | custom-call | tf_op jit(solution)/shard_map/sketch/pallas_call | solution.py:508
  64.6 1.5 %copy.8 = f32[1,2,64,128]{3,1,2,0:T(2,128)} copy(f32[1,2,64,128]{3,2,1,0:T(8,128)} %bitcast.7) | data formatting | bytes 131072
